TPU v7x, 256 devices: a whole 4x4x8 slice. The times are simulated.
256 devices in a mesh: seq: 8 (over z_hi, core), expert: 16 (over y, x), tensor: 2 (over z_lo).
Axes of the slice: x: 4, y: 4, z: 8 (z_hi: 4, z_lo: 2; z = z_hi * 2 + z_lo), core: 2. Of those that a mesh axis runs over, the one named last changes fastest.
Arguments:
- q_rows: bfloat16 [16, 1024, 4096], P('expert', 'seq', 'tensor'), may hold values from -6 to 6
- k_rows: bfloat16 [16, 1024, 512], P('expert', 'seq', 'tensor'), may hold values from -6 to 6
- value_rows: bfloat16 [16, 1024, 512], P('expert', 'seq', 'tensor'), may hold values from -6 to 6
- x_rows: bfloat16 [16, 1024, 2048], P('expert', 'seq'), may hold values from -40 to 40
- out_weight: bfloat16 [4096, 2048], P('tensor', 'expert'), may hold values from -0.09375 to 0.09375
- norm_gain: float32 [2048], P('tensor'), may hold values from 0.1 to 1.9
- w_gate: bfloat16 [128, 2048, 768], P(('seq', 'expert'), None, 'tensor'), may hold values from -0.125 to 0.125
- w_up: bfloat16 [128, 2048, 768], P(('seq', 'expert'), None, 'tensor'), may hold values from -0.125 to 0.125
- w_down: bfloat16 [128, 768, 2048], P(('seq', 'expert'), 'tensor'), may hold values from -0.21875 to 0.21875
- expert_ids: int32 [16, 1024, 8], P('expert', 'seq'), may hold values from 0 to 127, all different within a row; in each aligned block of 128 rows (0 to 127, 128 to 255, ..., all dimensions but the last counted through in order) at most 12 rows name the same one
- gate_weights: float32 [16, 1024, 8], P('expert', 'seq'), may hold values from 0.02 to 0.4
Outputs:
- layer_out: bfloat16 [16, 1024, 2048], P('expert', 'seq', 'tensor')
Inputs may be any that keep to these rules, and one draw needn't show every extreme that they name: `expert_ids`: in each token's row the 8 ids differ. Among the 128 tokens of one block of positions (the blocks laid session after session) no expert is named more than 12 times, a bound that some block reaches; every expert is named somewhere.
All inputs are finite; a program needn't handle non-finite values.
Results may differ from a plain program's by a relative error of at most 0.007.
Values may be sent and summed in bfloat16 or wider, within the bound.
A program may use at most 128 MiB of HBM per device.

v0:
```python
import math

import jax
import jax.numpy as jnp
from jax import lax
from jax.sharding import PartitionSpec as P

HEAD_SIZE = 128
TOPK = 8


def in_one_piece(arrays, axis, dim, along):
    widths = [a.shape[along] for a in arrays]
    both = jnp.concatenate(arrays, axis=along)
    out = lax.all_gather(both, axis, axis=dim, tiled=True)
    return tuple(jnp.split(out, [sum(widths[:k]) for k in range(1, len(widths))], axis=along))


def split_up(shard, dim, devices):
    before, after = (shard.shape[:dim], shard.shape[dim + 1 :])
    return jnp.moveaxis(shard.reshape(*before, devices, -1, *after), dim, 0)


def summed_on_arrival(shard, axis, dim):
    devices = lax.axis_size(axis)
    blocks = lax.all_to_all(split_up(shard, dim, devices), axis, 0, 0, tiled=True)
    return jnp.sum(blocks.astype(jnp.float32), axis=0)


def copy_for_each(shard, axis):
    copies = jnp.broadcast_to(shard, (lax.axis_size(axis), *shard.shape))
    return lax.all_to_all(copies, axis, split_axis=0, concat_axis=0, tiled=True)


def taken_together(shard, axis):
    everything = copy_for_each(shard, axis)
    return jnp.sum(everything, axis=0)


def joined_along(blocks, dim):
    blocks = jnp.moveaxis(blocks, 0, dim)
    dims = blocks.shape
    return blocks.reshape(*dims[:dim], dims[dim] * dims[dim + 1], *dims[dim + 2 :])


def one_exchange(shard, axis, axes, splits, concats):
    sizes = [lax.axis_size(a) for a in axes]
    blocks = split_up(shard, splits[0], sizes[0])
    blocks = jnp.moveaxis(split_up(blocks, splits[1] + 1, sizes[1]), 0, 1)
    inside = blocks.shape[2:]
    blocks = blocks.reshape(-1, *inside)
    blocks = lax.all_to_all(blocks, axis, split_axis=0, concat_axis=0, tiled=True)
    blocks = joined_along(blocks.reshape(*sizes, *inside), concats[0] + 1)
    return joined_along(blocks, concats[1])


def collect(shard, axis, dim):
    return joined_along(copy_for_each(shard, axis), dim)


def per_device(
    q_rows,
    k_rows,
    value_rows,
    x_rows,
    out_weight,
    norm_gain,
    w_gate,
    w_up,
    w_down,
    expert_ids,
    gate_weights,
):
    rows_here = q_rows.shape[1]
    kv_heads = k_rows.shape[2] // HEAD_SIZE
    q_heads = q_rows.shape[2] // HEAD_SIZE
    group_width = q_heads // kv_heads
    queries = q_rows[0].reshape(rows_here, kv_heads, group_width, HEAD_SIZE)
    offset = lax.axis_index("seq") * rows_here
    query_pos = offset + jnp.arange(rows_here, dtype=jnp.int32)
    softmax_scale = 1.0 / math.sqrt(HEAD_SIZE)
    tensor_pos = lax.axis_index("tensor")
    tensor_count = lax.axis_size("tensor")
    full_gate, full_up = in_one_piece((w_gate[0], w_up[0]), "tensor", 1, 0)
    full_down = lax.all_gather(w_down[0], "tensor", axis=0, tiled=True)
    pieces = in_one_piece((k_rows, value_rows), "seq", 1, 0)
    running_max = jnp.full((kv_heads, group_width, rows_here), -1e30, jnp.float32)
    block_rows = pieces[0].shape[1]
    key_block = pieces[0][0].reshape(block_rows, kv_heads, HEAD_SIZE)
    value_block = pieces[1][0].reshape(block_rows, kv_heads, HEAD_SIZE)
    scores = (
        jnp.einsum("igrd,jgd->grij", queries, key_block, preferred_element_type=jnp.float32)
        * softmax_scale
    )
    key_pos = jnp.arange(block_rows, dtype=jnp.int32)
    allowed = key_pos[None, :] <= query_pos[:, None]
    scores = jnp.where(allowed, scores, jnp.float32(-1e30))
    new_max = jnp.maximum(running_max, jnp.max(scores, axis=-1))
    weights = jnp.where(allowed, jnp.exp(scores - new_max[..., None]), jnp.float32(0.0))
    running_sum = jnp.sum(weights, axis=-1)
    weighted = jnp.einsum(
        "grij,jgd->grid",
        weights.astype(jnp.bfloat16),
        value_block,
        preferred_element_type=jnp.float32,
    )
    running_max, running_sum, weighted = (new_max, running_sum, weighted)
    attn_rows = (
        (weighted / running_sum[..., None])
        .transpose(2, 0, 1, 3)
        .reshape(rows_here, q_heads * HEAD_SIZE)
        .astype(jnp.bfloat16)
    )
    head_terms = jnp.dot(
        attn_rows,
        lax.all_gather(out_weight, "expert", axis=1, tiled=True),
        preferred_element_type=jnp.float32,
    )
    width = x_rows.shape[2]
    half_width = width // tensor_count
    share_sum = summed_on_arrival(head_terms.astype(jnp.bfloat16), "tensor", 1)
    mixed_half = (
        lax.dynamic_slice_in_dim(x_rows[0], tensor_pos * half_width, half_width, 1).astype(
            jnp.float32
        )
        + share_sum
    )
    power = taken_together(jnp.sum(mixed_half * mixed_half, axis=1), "tensor")
    inverse = lax.rsqrt(power / width + 1e-06)
    normed = (mixed_half * inverse[:, None] * norm_gain[None, :]).astype(jnp.bfloat16)
    seq_count = lax.axis_size("seq")
    group_count = lax.axis_size("expert")
    experts = seq_count * group_count
    capacity = max(2, 3 * rows_here * TOPK // (2 * experts))
    routed = expert_ids[0].reshape(-1)
    assigned = routed.shape[0]
    member = (routed[:, None] == jnp.arange(experts, dtype=jnp.int32)[None, :]).astype(jnp.int32)
    earlier = jnp.cumsum(member, axis=0) - member
    slot_index = jnp.sum(earlier * member, axis=1)
    target = routed * capacity + slot_index
    owner_index = (
        jnp.full((experts * capacity,), assigned, jnp.int32)
        .at[target]
        .set(jnp.arange(assigned, dtype=jnp.int32))
    )
    filled = owner_index < assigned
    source = jnp.minimum(owner_index // TOPK, rows_here - 1)
    whole_normed = collect(normed, "tensor", 1)
    outgoing = jnp.where(
        filled[:, None], whole_normed[source], jnp.zeros((), jnp.bfloat16)
    ).reshape(experts, capacity, width)
    half_cap = capacity // tensor_count
    my_slots = lax.dynamic_slice_in_dim(outgoing, tensor_pos * half_cap, half_cap, 1)
    hidden_half = full_down.shape[0] // tensor_count
    grouped = my_slots.reshape((seq_count, group_count) + my_slots.shape[1:])
    arrived = one_exchange(grouped, ("seq", "expert"), ("seq", "expert"), (0, 1), (0, 1))
    whole_arrived = arrived.reshape((experts,) + my_slots.shape[1:])
    flat_rows = whole_arrived.reshape(-1, width)
    gate_act = jnp.dot(flat_rows, full_gate, preferred_element_type=jnp.float32)
    up_act = jnp.dot(flat_rows, full_up, preferred_element_type=jnp.float32)
    hidden = (jax.nn.silu(gate_act) * up_act).astype(jnp.bfloat16)
    total = jnp.zeros((flat_rows.shape[0], width), jnp.float32)
    for group_pos in range(tensor_count):
        lo_col = group_pos * hidden_half
        piece = jnp.dot(
            hidden[:, lo_col : lo_col + hidden_half],
            full_down[lo_col : lo_col + hidden_half],
            preferred_element_type=jnp.float32,
        )
        total = total + piece.astype(jnp.bfloat16).astype(jnp.float32)
    finished = total.astype(jnp.bfloat16).reshape(whole_arrived.shape)
    finished = finished.reshape((seq_count, group_count) + finished.shape[1:])
    returned = one_exchange(finished, ("seq", "expert"), ("seq", "expert"), (0, 1), (0, 1))
    back_whole = returned.reshape((experts,) + returned.shape[2:])
    returned = lax.all_to_all(back_whole, "tensor", split_axis=2, concat_axis=1, tiled=True)
    came_back = returned.reshape(experts * capacity, half_width)
    picked = came_back[target].astype(jnp.float32)
    weights_flat = gate_weights[0].reshape(-1)
    blended = jnp.sum((picked * weights_flat[:, None]).reshape(rows_here, TOPK, half_width), axis=1)
    return (mixed_half + blended).astype(jnp.bfloat16)[None]


def solution(mesh):
    return jax.shard_map(
        per_device,
        mesh=mesh,
        in_specs=(
            P("expert", "seq", "tensor"),
            P("expert", "seq", "tensor"),
            P("expert", "seq", "tensor"),
            P("expert", "seq", None),
            P("tensor", "expert"),
            P("tensor"),
            P(("seq", "expert"), None, "tensor"),
            P(("seq", "expert"), None, "tensor"),
            P(("seq", "expert"), "tensor", None),
            P("expert", "seq", None),
            P("expert", "seq", None),
        ),
        out_specs=P("expert", "seq", "tensor"),
        check_vma=False,
    )
```

profile of v0, /device:TPU:32, one launch (start us, length us, event | category | flops | bytes accessed | tf_op | source)
XLA Modules:
  0.0 553.1 jit_solution(8807647525143231353)
XLA Ops:
  6.5 0.9 copy.93
  7.5 1.0 copy.94
  8.5 0.7 pad_maximum_fusion.1
  9.2 0.7 all-gather.8.cloned.1.call-update
  10.0 3.9 pad_maximum_fusion
  14.3 0.1 copy.119
  14.6 0.2 fusion.28
  14.8 26.3 %all-gather.6.cloned.1.call-done = bf16[2,1024,256]{1,2,0:T(8,128)(2,1)} async-done(((bf16[2,128,256]{1,2,0:T(8,128)(2,1)}), bf16[2,1024,256]{1,2,0:T(8,128)(2,1)}) %all-gather.6.cloned.1.call-update) | async-done | bytes 1048592 | tf_op jit(solution)/shard_map/all_gather | solution.py:15
  41.1 1.3 fusion.39
  42.4 1.5 fusion
  43.9 2.0 fusion.1
  45.9 2.1 divide_convert_fusion
  48.1 79.9 %all-gather.8.cloned.1.call-done = bf16[2048,2048]{1,0:T(8,128)(2,1)} async-done(((bf16[2048,128]{1,0:T(8,128)(2,1)}), bf16[2048,2048]{1,0:T(8,128)(2,1)}) %all-gather.8.cloned.1.call-update) | async-done | bytes 8388624 | tf_op jit(solution)/shard_map/all_gather | solution.py:116
  128.0 4.7 convolution_convert_fusion.2
  132.7 0.8 copy.125
  133.5 4.0 all-to-all-start
  137.8 0.4 fusion.25
  138.2 4.9 all-to-all-done
  143.2 0.2 multiply_reduce_fusion
  143.4 0.6 broadcast_in_dim.55
  144.0 4.9 all-to-all-start.1
  148.9 4.3 scatter_custom_fusion
  153.3 0.1 multiply_convert_fusion.1
  153.4 0.9 broadcast_in_dim.56
  154.3 3.7 all-to-all-start.2
  158.0 0.1 broadcast_in_dim.53
  158.2 11.8 %all-to-all-done.2 = bf16[2,128,1024]{2,1,0:T(8,128)(2,1)S(1)} async-done(((bf16[2,128,1024]{2,1,0:T(8,128)(2,1)}), bf16[2,128,1024]{2,1,0:T(8,128)(2,1)S(1)}, u32[]{:S(2)}, u32[]{:S(2)}) %all-to-all-start.2) | async-done | bytes 524320 | tf_op jit(solution)/shard_map/all_to_all | solution.py:32
  170.1 7.1 %gather_fusion = bf16[1536,2048]{1,0:T(8,128)(2,1)} fusion(bf16[128,2048]{1,0:T(8,128)(2,1)S(1)} %bitcast.108, s32[2048]{0:T(1024)S(1)} %pad_clamp_fusion), kind=kCustom, calls=%fused_computation | custom fusion | bytes 12589056 | tf_op jit(solution)/shard_map/gather | solution.py:150
  177.1 10.6 %gather.9 = bf16[128,12,2048]{2,1,0:T(8,128)(2,1)} reshape(bf16[1536,2048]{1,0:T(8,128)(2,1)} %gather_fusion) | data formatting | bytes 12582912 | tf_op jit(solution)/shard_map/gather | solution.py:150
  187.8 6.0 %fusion.3 = bf16[128,1,1,6,2048]{4,3,2,1,0:T(8,128)(2,1)} fusion(bf16[128,12,2048]{2,1,0:T(8,128)(2,1)} %gather.9, s32[]{:T(128)S(6)} %select_n.44, pred[128,6]{1,0:T(8,128)(4,1)S(1)} %constant_dynamic-slice_fusion), kind=kLoop, calls=%fused_computation.10 | loop fusion | flops 1572864 | bytes 6292228 | tf_op jit(solution)/shard_map/reshape;transpose;transpose;reshape;reshape;reshape | solution.py:51
  193.7 12.8 %all-to-all-start.3 = ((bf16[128,1,1,6,2048]{4,3,2,1,0:T(8,128)(2,1)}), bf16[128,1,1,6,2048]{4,3,2,1,0:T(8,128)(2,1)}, u32[]{:S(2)}, u32[]{:S(2)}) async-start(bf16[128,1,1,6,2048]{4,3,2,1,0:T(8,128)(2,1)} %fusion.3), calls=%async_computation.3 | async-start | bytes 8388608 | tf_op jit(solution)/shard_map/all_to_all | solution.py:52
  206.6 0.5 all-gather.12.cloned.1.call-update
  207.1 129.1 %all-to-all-done.3 = bf16[128,1,1,6,2048]{4,3,2,1,0:T(8,128)(2,1)} async-done(((bf16[128,1,1,6,2048]{4,3,2,1,0:T(8,128)(2,1)}), bf16[128,1,1,6,2048]{4,3,2,1,0:T(8,128)(2,1)}, u32[]{:S(2)}, u32[]{:S(2)}) %all-to-all-start.3) | async-done | bytes 3145760 | tf_op jit(solution)/shard_map/all_to_all | solution.py:52
  336.2 4.9 reshape_reshape_reshape.3
  341.1 4.6 fusion.10
  345.7 3.8 multiply_convert_fusion
  349.5 3.5 convolution_convert_fusion
  353.1 1.8 add_convert_fusion
  354.9 2.9 reshape_transpose_transpose_reshape_reshape_reshape_reshape.3
  357.7 83.6 %all_to_all.41 = bf16[128,1,1,6,2048]{4,3,2,1,0:T(8,128)(2,1)} all-to-all(bf16[128,1,1,6,2048]{4,3,2,1,0:T(8,128)(2,1)} %bitcast.109), channel_id=1, replica_groups=mesh['seq'=8,'expert'=16,'tensor'=2] {'seq','expert'}, dimensions={0} | all-to-all | bytes 6291456 | tf_op jit(solution)/shard_map/all_to_all | solution.py:52
  441.3 7.2 %copy.108 = bf16[128,6,2048]{0,1,2:T(8,128)(2,1)} copy(bf16[128,6,2048]{2,1,0:T(8,128)(2,1)} %bitcast.111) | data formatting | bytes 6291456 | tf_op jit(solution)/shard_map/reshape;reshape | solution.py:174
  448.5 29.3 %all-to-all-start.5 = ((bf16[128,6,2048]{0,1,2:T(8,128)(2,1)}), bf16[128,6,2048]{0,1,2:T(8,128)(2,1)}, u32[]{:S(2)}, u32[]{:S(2)}) async-start(bf16[128,6,2048]{0,1,2:T(8,128)(2,1)} %copy.108), calls=%async_computation.5 | async-start | bytes 8388608 | tf_op jit(solution)/shard_map/all_to_all | solution.py:175
  478.0 46.1 %all-to-all-done.5 = bf16[128,6,2048]{0,1,2:T(8,128)(2,1)} async-done(((bf16[128,6,2048]{0,1,2:T(8,128)(2,1)}), bf16[128,6,2048]{0,1,2:T(8,128)(2,1)}, u32[]{:S(2)}, u32[]{:S(2)}) %all-to-all-start.5) | async-done | bytes 3145760 | tf_op jit(solution)/shard_map/all_to_all | solution.py:175
  524.1 7.4 %copy.109 = bf16[128,6,2,1024]{3,1,2,0:T(8,128)(2,1)} copy(bf16[128,6,2,1024]{0,1,3,2:T(8,128)(2,1)} %bitcast.35) | data formatting | bytes 6291456 | tf_op jit(solution)/shard_map/all_to_all | solution.py:175
  531.5 4.9 reshape.117
  536.4 5.3 gather_fusion.1
  541.7 2.9 fusion.4
  544.7 1.9 fusion.22
  (57 shorter events, 1.5 us)
Async XLA Ops:
  6.5 34.6 %all-gather.6.cloned.1.call-start = ((), (), s32[]{:S(2)}) async-start(), calls=%async_computation.6 | async-start | bytes 1179648 | tf_op jit(solution)/shard_map/all_gather | solution.py:15
  9.2 118.8 %all-gather.8.cloned.1.call-start = ((), (), s32[]{:S(2)}) async-start(), calls=%async_computation.7 | async-start | bytes 8912896 | tf_op jit(solution)/shard_map/all_gather | solution.py:116
  9.9 331.2 %all-gather.10.cloned.1.call-start = ((), (), s32[]{:S(2)}) async-start(), calls=%async_computation.8 | async-start | bytes 9437184 | tf_op jit(solution)/shard_map/all_gather | solution.py:15
  10.0 4.0 copy-start.4
  10.0 4.4 copy-start.2
  14.8 29.1 %copy-start.3 = (s32[128,9]{0,1:T(8,128)}, s32[128,9]{0,1:T(8,128)S(1)}, u32[]{:S(2)}) copy-start(s32[128,9]{0,1:T(8,128)S(1)} %reduce-window.9) | copy-start | bytes 13828
  128.0 9.5 %slice-start = ((s32[128,9]{0,1:T(8,128)}), s32[128,8]{0,1:T(8,128)S(1)}, s32[]{:S(2)}) async-start(s32[128,9]{0,1:T(8,128)} %copy-done.3), calls=%async_computation.10 | async-start | bytes 8192 | tf_op jit(solution)/shard_map/slice.1
  132.6 10.6 %copy-start.1 = (bf16[1,128,2048]{2,1,0:T(8,128)(2,1)S(1)}, bf16[1,128,2048]{2,1,0:T(8,128)(2,1)}, u32[]{:S(2)}) copy-start(bf16[1,128,2048]{2,1,0:T(8,128)(2,1)} %param.14) | copy-start | bytes 1572868
  132.7 20.6 %copy-start.5 = (f32[1024]{0:T(1024)S(1)}, f32[1024]{0:T(1024)}, u32[]{:S(2)}) copy-start(f32[1024]{0:T(1024)} %param.16) | copy-start | bytes 12292
  133.5 9.6 %all-to-all-start = ((bf16[2,128,1024]{2,1,0:T(8,128)(2,1)}), bf16[2,128,1024]{2,1,0:T(8,128)(2,1)S(1)}, u32[]{:S(2)}, u32[]{:S(2)}) async-start(bf16[2,128,1024]{2,1,0:T(8,128)(2,1)} %bitcast.107), calls=%async_computation | async-start | bytes 1048576 | tf_op jit(solution)/shard_map/all_to_all | solution.py:26
  143.2 26.8 %copy-start = (f32[128,1024]{1,0:T(8,128)}, f32[128,1024]{1,0:T(8,128)S(1)}, u32[]{:S(2)}) copy-start(f32[128,1024]{1,0:T(8,128)S(1)} %convert_reduce_fusion) | copy-start | bytes 1572868
  144.0 9.3 %all-to-all-start.1 = ((f32[2,1,128]{2,1,0:T(1,128)}), f32[2,1,128]{2,1,0:T(1,128)S(1)}, u32[]{:S(2)}, u32[]{:S(2)}) async-start(f32[2,1,128]{2,1,0:T(1,128)} %broadcast_in_dim.55), calls=%async_computation.1 | async-start | bytes 2048 | tf_op jit(solution)/shard_map/all_to_all | solution.py:32
  154.3 15.8 %all-to-all-start.2 = ((bf16[2,128,1024]{2,1,0:T(8,128)(2,1)}), bf16[2,128,1024]{2,1,0:T(8,128)(2,1)S(1)}, u32[]{:S(2)}, u32[]{:S(2)}) async-start(bf16[2,128,1024]{2,1,0:T(8,128)(2,1)} %broadcast_in_dim.56), calls=%async_computation.2 | async-start | bytes 1048576 | tf_op jit(solution)/shard_map/all_to_all | solution.py:32
  193.7 142.4 %all-to-all-start.3 = ((bf16[128,1,1,6,2048]{4,3,2,1,0:T(8,128)(2,1)}), bf16[128,1,1,6,2048]{4,3,2,1,0:T(8,128)(2,1)}, u32[]{:S(2)}, u32[]{:S(2)}) async-start(bf16[128,1,1,6,2048]{4,3,2,1,0:T(8,128)(2,1)} %fusion.3), calls=%async_computation.3 | async-start | bytes 8388608 | tf_op jit(solution)/shard_map/all_to_all | solution.py:52
  206.5 143.0 %all-gather.12.cloned.1.call-start = ((), (), s32[]{:S(2)}) async-start(), calls=%async_computation.9 | async-start | bytes 4718592 | tf_op jit(solution)/shard_map/all_gather | solution.py:85
  341.1 4.7 copy-start.7
  349.5 3.5 copy-start.8
  349.5 3.5 copy-start.9
  448.5 29.3 %copy-start.6 = (f32[1,128,8]{1,2,0:T(8,128)S(1)}, f32[1,128,8]{1,2,0:T(8,128)}, u32[]{:S(2)}) copy-start(f32[1,128,8]{1,2,0:T(8,128)} %param.21) | copy-start | bytes 12292
  448.5 75.6 %all-to-all-start.5 = ((bf16[128,6,2048]{0,1,2:T(8,128)(2,1)}), bf16[128,6,2048]{0,1,2:T(8,128)(2,1)}, u32[]{:S(2)}, u32[]{:S(2)}) async-start(bf16[128,6,2048]{0,1,2:T(8,128)(2,1)} %copy.108), calls=%async_computation.5 | async-start | bytes 8388608 | tf_op jit(solution)/shard_map/all_to_all | solution.py:175
Sparse Core Ops, SparseCore 0:
  9.3 31.8 all-gather.5
  43.5 84.4 all-gather.7
  129.8 128.9 all-gather.9
  260.4 82.2 all-gather.11
where the time goes:
time: 556 us; the launch traced here: 553 us
  waiting for transfers between devices  299 us (54%)
  blocking collectives  83.6 us (15%)
  local copies, waits for them, and re-layouts  61.2 us (11%)
  starting transfers between devices  54.8 us (10%)
  matrix products  22 us (4%)
  other arithmetic  18.6 us (3%)
  between operations  13.5 us (2%)
    all_to_all x1, waiting for transfers between devices, one_exchange(): lax.all_to_all(blocks, axis, split_axis=0, concat_axis=0, tiled=True)  129 us
    all_to_all x1, blocking collectives, one_exchange(): lax.all_to_all(blocks, axis, split_axis=0, concat_axis=0, tiled=True)  83.6 us
    all_gather x1, waiting for transfers between devices, per_device(): lax.all_gather(out_weight, 'expert', axis=1, tiled=True)  79.9 us
    all_to_all x1, waiting for transfers between devices, per_device(): lax.all_to_all(back_whole, 'tensor', split_axis=2, concat_axis=1, tiled=T...  46.1 us
    all_to_all x1, starting transfers between devices, per_device(): lax.all_to_all(back_whole, 'tensor', split_axis=2, concat_axis=1, tiled=T...  29.3 us
    all_gather x2, waiting for transfers between devices, in_one_piece(): out = lax.all_gather(both, axis, axis=dim, tiled=True)  26.3 us
    gather x2, local copies, waits for them, and re-layouts, per_device(): whole_normed[source]  17.7 us
    all_to_all x1, starting transfers between devices, one_exchange(): lax.all_to_all(blocks, axis, split_axis=0, concat_axis=0, tiled=True)  12.8 us
  transfers between devices with their start and end apart: 9, of which 6 were waited for; matrix products, arithmetic and copies ran while one was open for 11% of the time, Pallas kernels for 0%

commit v1 on v0

v1 whole, which is shorter than its diff:
```python
import math

import jax
import jax.numpy as jnp
from jax import lax
from jax.experimental import pallas as pl
from jax.experimental.pallas import tpu as pltpu
from jax.sharding import PartitionSpec as P

MESH = pl.DeviceIdType.MESH
BF = jnp.bfloat16
F32 = jnp.float32

NX, NY, NZ = 4, 4, 8
NP = NX * NY
HEAD = 128
TOK = 128
HALF_TOK = 64
D = 2048
CAP = 12
NBLK = 4
MSG = NBLK * CAP
ROWS = NP * MSG
TOKS = NBLK * TOK
NF = 4
FC = D // NF
FFH = 384
FF = 768
HALF_D = D // 2
WROWS = 1024
ORDER = (0, 2, 1, 3)


def layer_kernel(
    q_h, k_h, v_h, x_h, w_h, gain_h, wg_h, wu_h, wd_h, ids_h, gat_h,
    out_ref,
    q_v, x_v, kv_v, w_v, gain_v, ids_v, gat_v,
    attn_v, ph_v, px_v, px2_v, mix_v, mixo_v,
    xg_v, p_v, gt_v, g_v, s_v, r_v,
    wg_v, wu_v, wd_v, ag_v, au_v, hid_v,
    y_v, yr_v, o_v, rs_s, rs_r,
    loc, hk, hz, wz_s, wk_s, wf_s,
    kv_s, kv_r, kvc_s, kvc_r, kv2_s, kv2_r,
    sm_s, sm_r,
    wa_s, wa_r, wa2_r, wb_s, wb_r, wb2_r, wc_s, wc_r,
    px_s, px_r, px2_s, px2_r,
    xg_s, xg_r, dsp_s, dsp_r, dsp_l, ret_s, ret_r, ret_l,
    rs_ss, rs_rs,
):
    rem, div = lax.rem, lax.div
    s = lax.axis_index("seq")
    e = lax.axis_index("expert")
    t = lax.axis_index("tensor")
    zh = div(s, 2)
    c = rem(s, 2)
    z = zh * 2 + t
    y = div(e, NX)
    x = rem(e, NX)
    oc = 1 - c
    giver = rem(c + t, 2)

    def dev(zz, ee, cc):
        return (div(zz, 2) * 2 + cc, ee, rem(zz, 2))

    def zmod(v):
        return rem(v + NZ, NZ)

    def send(src, dst, ss, rs, who):
        cp = pltpu.make_async_remote_copy(
            src_ref=src, dst_ref=dst, send_sem=ss, recv_sem=rs, device_id=who, device_id_type=MESH
        )
        cp.start()

    def local(src, dst, sem):
        pltpu.make_async_copy(src, dst, sem).start()

    def wait(ref, sem):
        pltpu.make_async_copy(ref, ref, sem).wait()

    def m8(v, n):
        return pl.multiple_of(v, n)

    other = dev(z, e, oc)
    partner = dev(z + 1 - 2 * t, e, c)
    cross = dev(z + 1 - 2 * t, e, oc)
    z_next, z_prev = dev(zmod(z + 1), e, c), dev(zmod(z - 1), e, c)
    zh_next, zh_prev = dev(zmod(z + 2), e, c), dev(zmod(z - 2), e, c)
    zh_opp = dev(zmod(z + 4), e, c)

    def plane_peer(k):
        return rem(y + div(k, NX), NY) * NX + rem(x + rem(k, NX), NX)

    a = (1 - c) * x + c * y
    b = (1 - c) * y + c * x

    def blk(ao, bo):
        aa, bb = rem(a + ao, 4), rem(b + bo, 4)
        return (1 - c) * (bb * 4 + aa) + c * (aa * 4 + bb)

    def frame_dev(ao, bo):
        return dev(z, blk(ao, bo), c)

    wrow = m8(c * WROWS, WROWS)
    a_next, a_prev = frame_dev(1, 0), frame_dev(3, 0)
    b_next, b_prev = frame_dev(0, 1), frame_dev(0, 3)
    OFF = (0, 3, 1, 2)

    own_kv = kv_v.at[s]
    local(k_h, kv_v.at[s, 0], loc.at[0])
    local(v_h, kv_v.at[s, 1], loc.at[1])
    local(w_h, w_v.at[e], loc.at[2])
    local(q_h, q_v, loc.at[3])
    local(x_h, x_v, loc.at[4])
    gcol = m8(t * HALF_D, HALF_D)
    local(gain_h, gain_v.at[:, pl.ds(gcol, HALF_D)], loc.at[5])
    icol = m8(zh * TOK, TOK)
    local(ids_h, ids_v.at[:, pl.ds(icol, TOK)], loc.at[6])
    local(gat_h, gat_v.at[:, pl.ds(icol, TOK)], loc.at[7])

    barrier = pltpu.get_barrier_semaphore()

    def greet(who):
        pl.semaphore_signal(barrier, inc=1, device_id=who, device_id_type=MESH)

    for who in (other, partner, cross, zh_next, zh_prev, zh_opp):
        greet(who)
    greet(dev(zmod(z - 1 + 2 * t), e, c))

    def greet_plane(k, carry):
        greet(dev(z, plane_peer(k), c))
        return carry

    lax.fori_loop(1, NP, greet_plane, 0)
    wait(kv_v.at[s, 0], loc.at[0])
    wait(kv_v.at[s, 1], loc.at[1])
    wait(w_v.at[e], loc.at[2])
    wait(gain_v.at[:, pl.ds(gcol, HALF_D)], loc.at[5])
    wait(ids_v.at[:, pl.ds(icol, TOK)], loc.at[6])
    wait(gat_v.at[:, pl.ds(icol, TOK)], loc.at[7])
    pl.semaphore_wait(barrier, 7 + NP - 1)

    send(own_kv, own_kv, kv_s.at[0], kv_r.at[0], zh_next)
    send(own_kv, own_kv, kv_s.at[1], kv_r.at[1], zh_prev)
    send(own_kv, own_kv, kvc_s.at[0], kvc_r.at[0], other)
    for n, who in enumerate((zh_next, zh_prev, zh_opp)):
        ids_mine = ids_v.at[:, pl.ds(icol, TOK)]
        gat_mine = gat_v.at[:, pl.ds(icol, TOK)]
        send(ids_mine, ids_mine, sm_s.at[n], sm_r.at[n], who)
        send(gat_mine, gat_mine, sm_s.at[3 + n], sm_r.at[3 + n], who)
    gain_mine = gain_v.at[:, pl.ds(gcol, HALF_D)]
    send(gain_mine, gain_mine, sm_s.at[6], sm_r.at[6], partner)

    def wpart(i, row0, rows):
        return w_v.at[i, pl.ds(m8(wrow + row0, 512), rows), :]

    mine = wpart(blk(0, 0), 0, WROWS)
    send(mine, mine, wa_s, wa_r.at[0], a_next)
    send(mine, mine, wa_s, wa_r.at[1], a_prev)
    send(mine, mine, wb_s, wb_r.at[0, 0], b_next)
    send(mine, mine, wb_s, wb_r.at[0, 1], b_prev)

    def on_chip(i):
        part = wpart(i, 0, WROWS)
        send(part, part, wc_s, wc_r, other)

    def spread_b(n):
        part = wpart(blk(OFF[n], 0), 0, WROWS)
        send(part, part, wb_s, wb_r.at[n, 0], b_next)
        send(part, part, wb_s, wb_r.at[n, 1], b_prev)

    hcol = m8(t * FFH, 128)
    gcolz = m8((1 - t) * FFH, 128)

    @pl.when(giver == 0)
    def _():
        for n, (src, dst) in enumerate(
            (
                (wg_h, wg_v.at[:, pl.ds(hcol, FFH)]),
                (wu_h, wu_v.at[:, pl.ds(hcol, FFH)]),
                (wd_h, wd_v.at[pl.ds(hcol, FFH), :]),
            )
        ):
            local(src, dst, hk.at[n])
            send(src, dst, wk_s.at[n], hk.at[n], other)

    left_kv = kv_v.at[rem(zh + 3, 4) * 2 + c]
    right_kv = kv_v.at[rem(zh + 1, 4) * 2 + c]
    opp = rem(zh + 2, 4) * 2 + c
    wait(own_kv, kv_r.at[0])
    send(left_kv.at[0], left_kv.at[0], kv2_s.at[0], kv2_r.at[0], zh_next)
    send(left_kv, left_kv, kvc_s.at[1], kvc_r.at[1], other)
    wait(own_kv, kv_r.at[1])
    send(right_kv.at[1], right_kv.at[1], kv2_s.at[1], kv2_r.at[1], zh_prev)
    send(right_kv, right_kv, kvc_s.at[2], kvc_r.at[2], other)

    wait(mine, wa_r.at[0])
    part = wpart(blk(3, 0), 0, 512)
    send(part, part, wa_s, wa2_r.at[0], a_next)
    wait(mine, wa_r.at[1])
    part = wpart(blk(1, 0), 512, 512)
    send(part, part, wa_s, wa2_r.at[1], a_prev)
    spread_b(1)
    spread_b(2)
    on_chip(blk(3, 0))
    on_chip(blk(1, 0))

    wait(kv_v.at[opp, 0], kv2_r.at[0])
    wait(kv_v.at[opp, 1], kv2_r.at[1])
    send(kv_v.at[opp], kv_v.at[opp], kvc_s.at[3], kvc_r.at[3], other)

    def wchunks(h):
        col = m8(h * FFH, 128)
        out = []
        for f in range(NF):
            out.append((wg_h.at[pl.ds(f * FC, FC), :], wg_v.at[pl.ds(f * FC, FC), pl.ds(col, FFH)]))
            out.append((wu_h.at[pl.ds(f * FC, FC), :], wu_v.at[pl.ds(f * FC, FC), pl.ds(col, FFH)]))
        for f in ORDER:
            out.append((wd_h.at[:, pl.ds(f * FC, FC)], wd_v.at[pl.ds(col, FFH), pl.ds(f * FC, FC)]))
        return out

    mine_chunks = wchunks(t)
    their_chunks = wchunks(1 - t)

    @pl.when(giver == 1)
    def _():
        for n, (src, dst) in enumerate(mine_chunks):
            send(src, dst, wz_s.at[n], hz.at[n], cross)

    def weights_in(n):
        dst = their_chunks[n][1]
        wait(dst, hz.at[n])

        @pl.when(giver == 1)
        def _():
            send(dst, dst, wf_s.at[n], hz.at[n], other)

    wait(wpart(blk(2, 0), 0, 512), wa2_r.at[0])
    wait(wpart(blk(2, 0), 512, 512), wa2_r.at[1])
    spread_b(3)
    on_chip(blk(2, 0))

    for n in range(3):
        wait(ids_v.at[:, pl.ds(icol, TOK)], sm_r.at[n])
        wait(gat_v.at[:, pl.ds(icol, TOK)], sm_r.at[3 + n])
    ids = ids_v[...]
    gates = gat_v[...]
    mine_ids = NP * z + lax.broadcasted_iota(jnp.int32, (NP, TOKS), 0)
    member = jnp.zeros((NP, TOKS), F32)
    gate_of = jnp.zeros((NP, TOKS), F32)
    for k in range(8):
        hit = ids[k : k + 1, :] == mine_ids
        member = jnp.where(hit, 1.0, member)
        gate_of = jnp.where(hit, gates[k : k + 1, :], gate_of)
    before = (
        lax.broadcasted_iota(jnp.int32, (TOK, TOK), 0) < lax.broadcasted_iota(jnp.int32, (TOK, TOK), 1)
    ).astype(BF)
    places = []
    for n in range(NBLK):
        mb = member[:, n * TOK : (n + 1) * TOK]
        rank = jnp.dot(mb.astype(BF), before, preferred_element_type=F32)
        places.append(jnp.where(mb > 0.5, rank + float(n * CAP), -1.0))
    place = jnp.concatenate(places, axis=1)
    row_id = lax.broadcasted_iota(jnp.int32, (MSG, TOKS), 0).astype(F32)
    for j in range(NP):
        hit = jnp.broadcast_to(place[j : j + 1, :], (MSG, TOKS)) == row_id
        p_v[j * MSG : (j + 1) * MSG, :] = jnp.where(hit, 1.0, 0.0).astype(BF)
        gt_v[j * MSG : (j + 1) * MSG, :] = jnp.where(
            hit, jnp.broadcast_to(gate_of[j : j + 1, :], (MSG, TOKS)), 0.0
        )
    for j in range(ROWS // 128):
        g_v[:, j * 128 : (j + 1) * 128] = gt_v[j * 128 : (j + 1) * 128, :].T.astype(BF)

    for n in range(4):
        wait(own_kv, kvc_r.at[n])
    wait(q_v, loc.at[3])
    softmax_scale = 1.0 / math.sqrt(HEAD)
    allowed = lax.broadcasted_iota(jnp.int32, (2 * TOK, 8 * TOK), 1) <= (
        s * TOK + rem(lax.broadcasted_iota(jnp.int32, (2 * TOK, 8 * TOK), 0), TOK)
    )

    def heads_pair(i, carry):
        g = div(i, 4)
        lane = m8(i * 256, 256)
        kl = m8(g * HEAD, HEAD)
        qq = jnp.concatenate(
            [q_v[:, pl.ds(lane, HEAD)], q_v[:, pl.ds(m8(lane + HEAD, HEAD), HEAD)]], axis=0
        )
        kk = kv_v[:, 0, :, pl.ds(kl, HEAD)].reshape(8 * TOK, HEAD)
        vv = kv_v[:, 1, :, pl.ds(kl, HEAD)].reshape(8 * TOK, HEAD)
        sc = lax.dot_general(qq, kk, (((1,), (1,)), ((), ())), preferred_element_type=F32)
        sc = jnp.where(allowed, sc * softmax_scale, -1e30)
        top = jnp.max(sc, axis=1, keepdims=True)
        p = jnp.exp(sc - top)
        tot = jnp.sum(p, axis=1, keepdims=True)
        o = jnp.dot(p.astype(BF), vv, preferred_element_type=F32) / tot
        o = o.astype(BF)
        attn_v[:, pl.ds(lane, HEAD)] = o[:TOK]
        attn_v[:, pl.ds(m8(lane + HEAD, HEAD), HEAD)] = o[TOK:]
        return carry

    def second_axis(n):
        wait(mine, wb_r.at[n, 0])
        fwd = wpart(blk(OFF[n], 3), 0, 512)
        send(fwd, fwd, wb_s, wb2_r.at[n, 0], b_next)
        on_chip(blk(OFF[n], 3))
        wait(mine, wb_r.at[n, 1])
        fwd = wpart(blk(OFF[n], 1), 512, 512)
        send(fwd, fwd, wb_s, wb2_r.at[n, 1], b_prev)
        on_chip(blk(OFF[n], 1))

    for grp in range(4):
        lax.fori_loop(2 * grp, 2 * grp + 2, heads_pair, 0)
        second_axis(grp)
    for n in range(4):
        wait(wpart(blk(OFF[n], 2), 0, 512), wb2_r.at[n, 0])
        wait(wpart(blk(OFF[n], 2), 512, 512), wb2_r.at[n, 1])
        on_chip(blk(OFF[n], 2))
    wait(w_v.at[pl.ds(0, 15), pl.ds(0, WROWS), :], wc_r)

    my_row = m8(t * HALF_TOK, HALF_TOK)
    their_row = m8((1 - t) * HALF_TOK, HALF_TOK)
    for f in range(NF):

        def project(i, carry):
            wb = f * 4 + i * 2
            ww = jnp.concatenate([w_v[wb], w_v[wb + 1]], axis=1)
            r = jnp.dot(attn_v[...], ww, preferred_element_type=F32)
            ph_v[f, :, pl.ds(m8(i * 256, 256), 256)] = r.astype(BF)
            return carry

        lax.fori_loop(0, 2, project, 0)
        send(ph_v.at[f, pl.ds(their_row, HALF_TOK), :], px_v.at[f], px_s.at[f], px_r.at[f], partner)
    their_f = (1 - t) * 2
    send(
        ph_v.at[pl.ds(their_f, 2), pl.ds(my_row, HALF_TOK), :], px2_v, px2_s, px2_r, partner
    )
    wait(x_v, loc.at[4])
    wait(gain_v.at[:, pl.ds(gcol, HALF_D)], sm_r.at[6])
    power = jnp.zeros((HALF_TOK, 1), F32)
    for f in range(NF):
        wait(px_v.at[f], px_r.at[f])
        mix = (
            x_v[pl.ds(my_row, HALF_TOK), f * FC : (f + 1) * FC].astype(F32)
            + ph_v[f, pl.ds(my_row, HALF_TOK), :].astype(F32)
            + px_v[f].astype(F32)
        )
        mix_v[f] = mix
        power = power + jnp.sum(mix * mix, axis=1, keepdims=True)
    inverse = lax.rsqrt(power / D + 1e-06)

    zrow = m8(z * HALF_TOK, HALF_TOK)
    for f in range(NF):
        gain = gain_v[:, f * FC : (f + 1) * FC]
        xg_v[f, pl.ds(zrow, HALF_TOK), :] = (mix_v[f] * inverse * gain).astype(BF)
        shard = xg_v.at[f, pl.ds(zrow, HALF_TOK), :]
        send(shard, shard, xg_s.at[0], xg_r.at[f, 0, 0], z_next)
        send(shard, shard, xg_s.at[1], xg_r.at[f, 1, 0], z_prev)

    def reach(f, d):
        return 4 if (f + d) % 2 == 0 else 3

    def ring_step(f, k):
        for d in range(2):
            if k > reach(f, d):
                continue
            src_z = zmod(z - k) if d == 0 else zmod(z + k)
            shard = xg_v.at[f, pl.ds(m8(src_z * HALF_TOK, HALF_TOK), HALF_TOK), :]
            wait(shard, xg_r.at[f, d, k - 1])
            if k + 1 <= reach(f, d):
                send(shard, shard, xg_s.at[d], xg_r.at[f, d, k], z_next if d == 0 else z_prev)

    my_slot = pl.ds(m8(e * MSG, 16), MSG)

    def exchange(buf, dst, f, ss, rs, ls):
        def one(k, carry):
            peer = plane_peer(k)
            send(
                buf.at[f, pl.ds(m8(peer * MSG, 16), MSG), :],
                dst.at[f, my_slot, :],
                ss.at[f],
                rs.at[f],
                dev(z, peer, c),
            )
            return carry

        lax.fori_loop(1, NP, one, 0)
        local(buf.at[f, my_slot, :], dst.at[f, my_slot, :], ls.at[f])

    FIFTEEN = (NP - 1) * MSG

    def exchanged(dst, f, rs, ls):
        wait(dst.at[f, pl.ds(0, FIFTEEN), :], rs.at[f])
        wait(dst.at[f, my_slot, :], ls.at[f])

    def pick_rows(f):
        def group(i, carry):
            rows = pl.ds(m8(i * 256, 256), 256)
            s_v[f, rows, :] = jnp.dot(p_v[rows, :], xg_v[f], preferred_element_type=F32).astype(BF)
            return carry

        lax.fori_loop(0, ROWS // 256, group, 0)
        exchange(s_v, r_v, f, dsp_s, dsp_r, dsp_l)

    for wave in range(1, NF + 4):
        for f in range(NF):
            k = wave - f
            if 1 <= k <= 4:
                ring_step(f, k)
                if k == 4:
                    pick_rows(f)

    wait(px2_v, px2_r)
    my_f = t * 2
    for u in range(2):
        cols = pl.ds(m8(gcol + u * FC, FC), FC)
        mixo_v[u, pl.ds(my_row, HALF_TOK), :] = mix_v[my_f + u]
        mixo_v[u, pl.ds(their_row, HALF_TOK), :] = (
            x_v[pl.ds(their_row, HALF_TOK), cols].astype(F32)
            + ph_v[my_f + u, pl.ds(their_row, HALF_TOK), :].astype(F32)
            + px2_v[u].astype(F32)
        )

    wait(wg_v.at[:, pl.ds(hcol, FFH)], hk.at[0])
    wait(wu_v.at[:, pl.ds(hcol, FFH)], hk.at[1])
    for f in range(NF):
        weights_in(2 * f)
        weights_in(2 * f + 1)
        exchanged(r_v, f, dsp_r, dsp_l)

        def gate_up(i, carry):
            rows = pl.ds(m8(i * 256, 256), 256)
            rr = r_v[f, rows, :]
            ga = jnp.dot(rr, wg_v[f * FC : (f + 1) * FC, :], preferred_element_type=F32)
            ua = jnp.dot(rr, wu_v[f * FC : (f + 1) * FC, :], preferred_element_type=F32)
            if f > 0:
                ga = ga + ag_v[rows, :]
                ua = ua + au_v[rows, :]
            if f < NF - 1:
                ag_v[rows, :] = ga
                au_v[rows, :] = ua
            else:
                hid_v[rows, :] = (ga / (1.0 + jnp.exp(-ga)) * ua).astype(BF)
            return carry

        lax.fori_loop(0, ROWS // 256, gate_up, 0)

    wait(wd_v.at[pl.ds(hcol, FFH), :], hk.at[2])
    for n, f in enumerate(ORDER):
        weights_in(8 + n)

        def down(i, carry):
            rows = pl.ds(m8(i * 256, 256), 256)
            cols = slice(f * FC, (f + 1) * FC)
            y0 = jnp.dot(hid_v[rows, :FFH], wd_v[:FFH, cols], preferred_element_type=F32)
            y1 = jnp.dot(hid_v[rows, FFH:], wd_v[FFH:, cols], preferred_element_type=F32)
            y_v[f, rows, :] = (y0.astype(BF).astype(F32) + y1.astype(BF).astype(F32)).astype(BF)
            return carry

        lax.fori_loop(0, ROWS // 256, down, 0)
        exchange(y_v, yr_v, f, ret_s, ret_r, ret_l)

    def combine(f):
        exchanged(yr_v, f, ret_r, ret_l)

        def group(i, carry):
            rows = pl.ds(m8(i * 256, 256), 256)
            o_v[f, rows, :] = jnp.dot(g_v[rows, :], yr_v[f], preferred_element_type=F32)
            return carry

        lax.fori_loop(0, TOKS // 256, group, 0)

    def own_part(dest, u):
        return o_v[rem(dest, 2) * 2 + u, pl.ds(m8(div(dest, 2) * TOK, TOK), TOK), :]

    def far(u, d):
        return 4 if (u + d) % 2 == 0 else 3

    def sum_step(u, i):
        for d in range(2):
            dist = far(u, d) - i
            if dist < 1:
                continue
            dest = zmod(z + dist) if d == 0 else zmod(z - dist)
            part = own_part(dest, u)
            if i > 0:
                slot = rs_r.at[u, d, dist]
                wait(slot, rs_rs.at[u, d, dist])
                part = part + rs_r[u, d, dist].astype(F32)
            rs_s[u, d, dist - 1] = part.astype(BF)
            send(
                rs_s.at[u, d, dist - 1],
                rs_r.at[u, d, dist - 1],
                rs_ss.at[u, d, dist - 1],
                rs_rs.at[u, d, dist - 1],
                z_next if d == 0 else z_prev,
            )

    def finish(u):
        for d in range(2):
            wait(rs_r.at[u, d, 0], rs_rs.at[u, d, 0])
        out_ref[:, u * FC : (u + 1) * FC] = (
            mixo_v[u]
            + (own_part(z, u) + rs_r[u, 0, 0].astype(F32) + rs_r[u, 1, 0].astype(F32))
        ).astype(BF)

    combine(0)
    combine(2)
    sum_step(0, 0)
    combine(1)
    sum_step(0, 1)
    combine(3)
    sum_step(1, 0)
    sum_step(0, 2)
    sum_step(1, 1)
    sum_step(0, 3)
    sum_step(1, 2)
    finish(0)
    sum_step(1, 3)
    finish(1)

    for n in range(2):
        wait(own_kv, kv_s.at[n])
        wait(own_kv.at[0], kv2_s.at[n])
    for n in range(4):
        wait(own_kv, kvc_s.at[n])
    for n in range(3):
        wait(ids_v.at[:, pl.ds(0, TOK)], sm_s.at[n])
        wait(gat_v.at[:, pl.ds(0, TOK)], sm_s.at[3 + n])
    wait(gain_mine, sm_s.at[6])
    wait(w_v.at[pl.ds(0, 3), pl.ds(0, WROWS), :], wa_s)
    wait(w_v.at[pl.ds(0, 12), pl.ds(0, WROWS), :], wb_s)
    wait(w_v.at[pl.ds(0, 15), pl.ds(0, WROWS), :], wc_s)
    for f in range(NF):
        wait(px_v.at[f], px_s.at[f])
        wait(s_v.at[f, pl.ds(0, FIFTEEN), :], dsp_s.at[f])
        wait(y_v.at[f, pl.ds(0, FIFTEEN), :], ret_s.at[f])
    wait(px2_v, px2_s)
    for d in range(2):
        wait(xg_v.at[pl.ds(0, 2), pl.ds(0, 7 * HALF_TOK), :], xg_s.at[d])
        for u in range(2):
            for n in range(far(u, d)):
                wait(rs_s.at[u, d, n], rs_ss.at[u, d, n])

    @pl.when(giver == 0)
    def _():
        wait(wg_h, wk_s.at[0])
        wait(wu_h, wk_s.at[1])
        wait(wd_h, wk_s.at[2])

    @pl.when(giver == 1)
    def _():
        for n in range(12):
            wait(mine_chunks[n][1], wz_s.at[n])
            wait(mine_chunks[n][1], wf_s.at[n])


def per_device(
    q_rows, k_rows, value_rows, x_rows, out_weight, norm_gain, w_gate, w_up, w_down, expert_ids, gate_weights
):
    dma = pltpu.SemaphoreType.DMA
    any_spec = pl.BlockSpec(memory_space=pl.ANY)
    out = pl.pallas_call(
        layer_kernel,
        out_shape=jax.ShapeDtypeStruct((TOK, HALF_D), BF),
        in_specs=[any_spec] * 11,
        out_specs=pl.BlockSpec(memory_space=pltpu.VMEM),
        scratch_shapes=[
            pltpu.VMEM((TOK, D), BF),
            pltpu.VMEM((TOK, D), BF),
            pltpu.VMEM((8, 2, TOK, 256), BF),
            pltpu.VMEM((NP, D, 128), BF),
            pltpu.VMEM((1, D), F32),
            pltpu.VMEM((8, TOKS), jnp.int32),
            pltpu.VMEM((8, TOKS), F32),
            pltpu.VMEM((TOK, D), BF),
            pltpu.VMEM((NF, TOK, FC), BF),
            pltpu.VMEM((NF, HALF_TOK, FC), BF),
            pltpu.VMEM((2, HALF_TOK, FC), BF),
            pltpu.VMEM((NF, HALF_TOK, FC), F32),
            pltpu.VMEM((2, TOK, FC), F32),
            pltpu.VMEM((NF, TOKS, FC), BF),
            pltpu.VMEM((ROWS, TOKS), BF),
            pltpu.VMEM((ROWS, TOKS), F32),
            pltpu.VMEM((TOKS, ROWS), BF),
            pltpu.VMEM((NF, ROWS, FC), BF),
            pltpu.VMEM((NF, ROWS, FC), BF),
            pltpu.VMEM((D, FF), BF),
            pltpu.VMEM((D, FF), BF),
            pltpu.VMEM((FF, D), BF),
            pltpu.VMEM((ROWS, FF), F32),
            pltpu.VMEM((ROWS, FF), F32),
            pltpu.VMEM((ROWS, FF), BF),
            pltpu.VMEM((NF, ROWS, FC), BF),
            pltpu.VMEM((NF, ROWS, FC), BF),
            pltpu.VMEM((NF, TOKS, FC), F32),
            pltpu.VMEM((2, 2, 4, TOK, FC), BF),
            pltpu.VMEM((2, 2, 4, TOK, FC), BF),
            dma((8,)), dma((3,)), dma((12,)), dma((12,)), dma((3,)), dma((12,)),
            dma((2,)), dma((2,)), dma((4,)), dma((4,)), dma((2,)), dma((2,)),
            dma((7,)), dma((7,)),
            dma, dma((2,)), dma((2,)), dma, dma((4, 2)), dma((4, 2)), dma, dma,
            dma((NF,)), dma((NF,)), dma, dma,
            dma((2,)), dma((NF, 2, 4)), dma((NF,)), dma((NF,)), dma((NF,)), dma((NF,)), dma((NF,)), dma((NF,)),
            dma((2, 2, 4)), dma((2, 2, 4)),
        ],
        compiler_params=pltpu.CompilerParams(
            collective_id=0, has_side_effects=True, vmem_limit_bytes=62 * 1024 * 1024
        ),
        name="layer",
    )(
        q_rows[0],
        k_rows[0],
        value_rows[0],
        x_rows[0],
        out_weight,
        norm_gain.reshape(1, HALF_D),
        w_gate[0],
        w_up[0],
        w_down[0],
        expert_ids[0].T,
        gate_weights[0].T,
    )
    return out[None]


def solution(mesh):
    return jax.shard_map(
        per_device,
        mesh=mesh,
        in_specs=(
            P("expert", "seq", "tensor"),
            P("expert", "seq", "tensor"),
            P("expert", "seq", "tensor"),
            P("expert", "seq", None),
            P("tensor", "expert"),
            P("tensor"),
            P(("seq", "expert"), None, "tensor"),
            P(("seq", "expert"), None, "tensor"),
            P(("seq", "expert"), "tensor", None),
            P("expert", "seq", None),
            P("expert", "seq", None),
        ),
        out_specs=P("expert", "seq", "tensor"),
        check_vma=False,
    )
```

time: 556 us -> 201 us (0.36)
  waiting for transfers between devices: 299 us -> 0 us
  Pallas kernels: 0 us -> 198 us
  blocking collectives: 83.6 us -> 0 us
  local copies, waits for them, and re-layouts: 61.2 us -> 1.67 us
  starting transfers between devices: 54.8 us -> 0 us
  matrix products: 22 us -> 0 us
  other arithmetic: 18.6 us -> 0 us
  between operations: 13.5 us -> 0.01 us
    pallas_call x0 -> x1, Pallas kernels: none -> 198 us  [per_device(): pl.pallas_call(layer_kernel, out_shape=jax.ShapeDtypeStruct((TOK, HALF_D)...]
    all_to_all x5 -> x0, waiting for transfers between devices: 192 us -> none  [the longest x1 129 us: one_exchange(): lax.all_to_all(blocks, axis, split_axis=0, concat_axis=0, tiled=True)]
    all_gather x4 -> x0, waiting for transfers between devices: 106 us -> none  [the longest x1 79.9 us: per_device(): lax.all_gather(out_weight, 'expert', axis=1, tiled=True)]
    all_to_all x1 -> x0, blocking collectives: 83.6 us -> none  [one_exchange(): lax.all_to_all(blocks, axis, split_axis=0, concat_axis=0, tiled=True)]
    all_to_all x5 -> x0, starting transfers between devices: 54.6 us -> none  [the longest x1 29.3 us: per_device(): lax.all_to_all(back_whole, 'tensor', split_axis=2, concat_axis=1, tiled=T...]
    gather x3 -> x0, local copies, waits for them, and re-layouts: 23 us -> none  [the longest x2 17.7 us: per_device(): whole_normed[source]]
    dot_general x7 -> x0, matrix products: 22 us -> none  [the longest x2 5.32 us: per_device(): jnp.dot(hidden[:, lo_col:lo_col + hidden_half], full_down[lo_col:lo_col +...]
    another operation x7 -> x0, local copies, waits for them, and re-layouts: 15 us -> none  [the longest x1 7.21 us: per_device(): back_whole = returned.reshape((experts,) + returned.shape[2:])]
  transfers between devices with their start and end apart: 9 -> 0, of which waited for: 6 -> 0; matrix products, arithmetic and copies ran while one was open for 11% -> 0% of each run, Pallas kernels for 0% -> 0%
where the time goes in v1:
time: 201 us; the launch traced here: 200 us
  Pallas kernels  198 us (99%)
    pallas_call x1, Pallas kernels, per_device(): pl.pallas_call(layer_kernel, out_shape=jax.ShapeDtypeStruct((TOK, HALF_D)...  198 us

profile of v1, /device:TPU:32, one launch (start us, length us, event | category | flops | bytes accessed | tf_op | source)
XLA Modules:
  0.0 199.9 jit_solution(4524961207262340193)
XLA Ops:
  0.0 198.3 %layer.1 = bf16[128,1024]{1,0:T(8,128)(2,1)} custom-call(bf16[128,2048]{1,0:T(8,128)(2,1)} %bitcast.19, bf16[128,256]{1,0:T(8,128)(2,1)} %bitcast.21, bf16[128,256]{1,0:T(8,128)(2,1)} %bitcast.22, bf16[128,2048]{1,0:T(8,128)(2,1)} %bitcast.20, bf16[2048,128]{1,0:T(8,128)(2,1)} %w_h.1, f32[1,1024]{1,0:T(1,128)} %bitcast.23, bf16[2048,384]{1,0:T(8,128)(2,1)} %bitcast.15, ...), custom_call_target="tpu_custom_call" | custom-call | tf_op jit(solution)/shard_map/layer/pallas_call | solution.py:562
  198.3 1.7 copy.13

commit v2 on v1

--- a/solution.py
+++ b/solution.py
@@ -28,7 +28,10 @@
 FF = 768
 HALF_D = D // 2
 WROWS = 1024
-ORDER = (0, 2, 1, 3)
+NR = 8
+RC = D // NR
+NU = NR // 2
+PAIRS = tuple(h * NU + u for u in range(NU) for h in range(2))
 
 
 def layer_kernel(
@@ -139,8 +142,12 @@
     wait(gat_v.at[:, pl.ds(icol, TOK)], loc.at[7])
     pl.semaphore_wait(barrier, 7 + NP - 1)
 
-    send(own_kv, own_kv, kv_s.at[0], kv_r.at[0], zh_next)
-    send(own_kv, own_kv, kv_s.at[1], kv_r.at[1], zh_prev)
+    def kv_part(i, n):
+        return kv_v.at[i, n]
+
+    for n in range(2):
+        send(kv_part(s, n), kv_part(s, n), kv_s.at[0, n], kv_r.at[0, n], zh_next)
+        send(kv_part(s, 1 - n), kv_part(s, 1 - n), kv_s.at[1, 1 - n], kv_r.at[1, 1 - n], zh_prev)
     send(own_kv, own_kv, kvc_s.at[0], kvc_r.at[0], other)
     for n, who in enumerate((zh_next, zh_prev, zh_opp)):
         ids_mine = ids_v.at[:, pl.ds(icol, TOK)]
@@ -183,15 +190,13 @@
             local(src, dst, hk.at[n])
             send(src, dst, wk_s.at[n], hk.at[n], other)
 
-    left_kv = kv_v.at[rem(zh + 3, 4) * 2 + c]
-    right_kv = kv_v.at[rem(zh + 1, 4) * 2 + c]
+    left = rem(zh + 3, 4) * 2 + c
+    right = rem(zh + 1, 4) * 2 + c
     opp = rem(zh + 2, 4) * 2 + c
-    wait(own_kv, kv_r.at[0])
-    send(left_kv.at[0], left_kv.at[0], kv2_s.at[0], kv2_r.at[0], zh_next)
-    send(left_kv, left_kv, kvc_s.at[1], kvc_r.at[1], other)
-    wait(own_kv, kv_r.at[1])
-    send(right_kv.at[1], right_kv.at[1], kv2_s.at[1], kv2_r.at[1], zh_prev)
-    send(right_kv, right_kv, kvc_s.at[2], kvc_r.at[2], other)
+    wait(kv_part(left, 0), kv_r.at[0, 0])
+    send(kv_part(left, 0), kv_part(left, 0), kv2_s.at[0], kv2_r.at[0], zh_next)
+    wait(kv_part(right, 1), kv_r.at[1, 1])
+    send(kv_part(right, 1), kv_part(right, 1), kv2_s.at[1], kv2_r.at[1], zh_prev)
 
     wait(mine, wa_r.at[0])
     part = wpart(blk(3, 0), 0, 512)
@@ -204,9 +209,10 @@
     on_chip(blk(3, 0))
     on_chip(blk(1, 0))
 
-    wait(kv_v.at[opp, 0], kv2_r.at[0])
-    wait(kv_v.at[opp, 1], kv2_r.at[1])
-    send(kv_v.at[opp], kv_v.at[opp], kvc_s.at[3], kvc_r.at[3], other)
+    wait(kv_part(left, 1), kv_r.at[0, 1])
+    send(kv_v.at[left], kv_v.at[left], kvc_s.at[1], kvc_r.at[1], other)
+    wait(kv_part(right, 0), kv_r.at[1, 0])
+    send(kv_v.at[right], kv_v.at[right], kvc_s.at[2], kvc_r.at[2], other)
 
     def wchunks(h):
         col = m8(h * FFH, 128)
@@ -214,17 +220,19 @@
         for f in range(NF):
             out.append((wg_h.at[pl.ds(f * FC, FC), :], wg_v.at[pl.ds(f * FC, FC), pl.ds(col, FFH)]))
             out.append((wu_h.at[pl.ds(f * FC, FC), :], wu_v.at[pl.ds(f * FC, FC), pl.ds(col, FFH)]))
-        for f in ORDER:
-            out.append((wd_h.at[:, pl.ds(f * FC, FC)], wd_v.at[pl.ds(col, FFH), pl.ds(f * FC, FC)]))
+        for f in PAIRS:
+            out.append((wd_h.at[:, pl.ds(f * RC, RC)], wd_v.at[pl.ds(col, FFH), pl.ds(f * RC, RC)]))
         return out
 
     mine_chunks = wchunks(t)
     their_chunks = wchunks(1 - t)
 
-    @pl.when(giver == 1)
-    def _():
-        for n, (src, dst) in enumerate(mine_chunks):
-            send(src, dst, wz_s.at[n], hz.at[n], cross)
+    def swap(lo, hi):
+        @pl.when(giver == 1)
+        def _():
+            for n in range(lo, hi):
+                src, dst = mine_chunks[n]
+                send(src, dst, wz_s.at[n], hz.at[n], cross)
 
     def weights_in(n):
         dst = their_chunks[n][1]
@@ -238,6 +246,28 @@
     wait(wpart(blk(2, 0), 512, 512), wa2_r.at[1])
     spread_b(3)
     on_chip(blk(2, 0))
+
+    def second_axis(n):
+        wait(mine, wb_r.at[n, 0])
+        fwd = wpart(blk(OFF[n], 3), 0, 512)
+        send(fwd, fwd, wb_s, wb2_r.at[n, 0], b_next)
+        on_chip(blk(OFF[n], 3))
+        wait(mine, wb_r.at[n, 1])
+        fwd = wpart(blk(OFF[n], 1), 512, 512)
+        send(fwd, fwd, wb_s, wb2_r.at[n, 1], b_prev)
+        on_chip(blk(OFF[n], 1))
+
+    def second_axis_end(n):
+        wait(wpart(blk(OFF[n], 2), 0, 512), wb2_r.at[n, 0])
+        wait(wpart(blk(OFF[n], 2), 512, 512), wb2_r.at[n, 1])
+        on_chip(blk(OFF[n], 2))
+
+    second_axis(0)
+
+    wait(kv_part(opp, 0), kv2_r.at[0])
+    wait(kv_part(opp, 1), kv2_r.at[1])
+    send(kv_v.at[opp], kv_v.at[opp], kvc_s.at[3], kvc_r.at[3], other)
+    swap(0, 4)
 
     for n in range(3):
         wait(ids_v.at[:, pl.ds(icol, TOK)], sm_r.at[n])
@@ -270,6 +300,7 @@
     for j in range(ROWS // 128):
         g_v[:, j * 128 : (j + 1) * 128] = gt_v[j * 128 : (j + 1) * 128, :].T.astype(BF)
 
+    second_axis(1)
     for n in range(4):
         wait(own_kv, kvc_r.at[n])
     wait(q_v, loc.at[3])
@@ -298,23 +329,17 @@
         attn_v[:, pl.ds(m8(lane + HEAD, HEAD), HEAD)] = o[TOK:]
         return carry
 
-    def second_axis(n):
-        wait(mine, wb_r.at[n, 0])
-        fwd = wpart(blk(OFF[n], 3), 0, 512)
-        send(fwd, fwd, wb_s, wb2_r.at[n, 0], b_next)
-        on_chip(blk(OFF[n], 3))
-        wait(mine, wb_r.at[n, 1])
-        fwd = wpart(blk(OFF[n], 1), 512, 512)
-        send(fwd, fwd, wb_s, wb2_r.at[n, 1], b_prev)
-        on_chip(blk(OFF[n], 1))
-
     for grp in range(4):
         lax.fori_loop(2 * grp, 2 * grp + 2, heads_pair, 0)
-        second_axis(grp)
-    for n in range(4):
-        wait(wpart(blk(OFF[n], 2), 0, 512), wb2_r.at[n, 0])
-        wait(wpart(blk(OFF[n], 2), 512, 512), wb2_r.at[n, 1])
-        on_chip(blk(OFF[n], 2))
+        if grp == 0:
+            second_axis(2)
+        if grp == 1:
+            second_axis_end(0)
+            second_axis(3)
+        if grp == 2:
+            second_axis_end(1)
+    second_axis_end(2)
+    second_axis_end(3)
     wait(w_v.at[pl.ds(0, 15), pl.ds(0, WROWS), :], wc_r)
 
     my_row = m8(t * HALF_TOK, HALF_TOK)
@@ -330,10 +355,6 @@
 
         lax.fori_loop(0, 2, project, 0)
         send(ph_v.at[f, pl.ds(their_row, HALF_TOK), :], px_v.at[f], px_s.at[f], px_r.at[f], partner)
-    their_f = (1 - t) * 2
-    send(
-        ph_v.at[pl.ds(their_f, 2), pl.ds(my_row, HALF_TOK), :], px2_v, px2_s, px2_r, partner
-    )
     wait(x_v, loc.at[4])
     wait(gain_v.at[:, pl.ds(gcol, HALF_D)], sm_r.at[6])
     power = jnp.zeros((HALF_TOK, 1), F32)
@@ -349,7 +370,7 @@
     inverse = lax.rsqrt(power / D + 1e-06)
 
     zrow = m8(z * HALF_TOK, HALF_TOK)
-    for f in range(NF):
+    def ring_open(f):
         gain = gain_v[:, f * FC : (f + 1) * FC]
         xg_v[f, pl.ds(zrow, HALF_TOK), :] = (mix_v[f] * inverse * gain).astype(BF)
         shard = xg_v.at[f, pl.ds(zrow, HALF_TOK), :]
@@ -401,13 +422,21 @@
         lax.fori_loop(0, ROWS // 256, group, 0)
         exchange(s_v, r_v, f, dsp_s, dsp_r, dsp_l)
 
+    ring_open(0)
+    ring_open(1)
     for wave in range(1, NF + 4):
         for f in range(NF):
-            k = wave - f
-            if 1 <= k <= 4:
-                ring_step(f, k)
-                if k == 4:
-                    pick_rows(f)
+            if 1 <= wave - f <= 4:
+                ring_step(f, wave - f)
+        if wave + 1 < NF:
+            ring_open(wave + 1)
+        if wave == NF + 3:
+            their_f = (1 - t) * 2
+            mid = ph_v.at[pl.ds(their_f, 2), pl.ds(my_row, HALF_TOK), :]
+            send(mid, px2_v, px2_s, px2_r, partner)
+            swap(4, 8 + NR)
+        if wave >= 4:
+            pick_rows(wave - 4)
 
     wait(px2_v, px2_r)
     my_f = t * 2
@@ -445,12 +474,12 @@
         lax.fori_loop(0, ROWS // 256, gate_up, 0)
 
     wait(wd_v.at[pl.ds(hcol, FFH), :], hk.at[2])
-    for n, f in enumerate(ORDER):
+    for n, f in enumerate(PAIRS):
         weights_in(8 + n)
 
         def down(i, carry):
             rows = pl.ds(m8(i * 256, 256), 256)
-            cols = slice(f * FC, (f + 1) * FC)
+            cols = slice(f * RC, (f + 1) * RC)
             y0 = jnp.dot(hid_v[rows, :FFH], wd_v[:FFH, cols], preferred_element_type=F32)
             y1 = jnp.dot(hid_v[rows, FFH:], wd_v[FFH:, cols], preferred_element_type=F32)
             y_v[f, rows, :] = (y0.astype(BF).astype(F32) + y1.astype(BF).astype(F32)).astype(BF)
@@ -470,7 +499,7 @@
         lax.fori_loop(0, TOKS // 256, group, 0)
 
     def own_part(dest, u):
-        return o_v[rem(dest, 2) * 2 + u, pl.ds(m8(div(dest, 2) * TOK, TOK), TOK), :]
+        return o_v[rem(dest, 2) * NU + u, pl.ds(m8(div(dest, 2) * TOK, TOK), TOK), :]
 
     def far(u, d):
         return 4 if (u + d) % 2 == 0 else 3
@@ -498,29 +527,31 @@
     def finish(u):
         for d in range(2):
             wait(rs_r.at[u, d, 0], rs_rs.at[u, d, 0])
-        out_ref[:, u * FC : (u + 1) * FC] = (
-            mixo_v[u]
+        lo = (u % 2) * RC
+        out_ref[:, u * RC : (u + 1) * RC] = (
+            mixo_v[u // 2, :, lo : lo + RC]
             + (own_part(z, u) + rs_r[u, 0, 0].astype(F32) + rs_r[u, 1, 0].astype(F32))
         ).astype(BF)
 
-    combine(0)
-    combine(2)
-    sum_step(0, 0)
-    combine(1)
-    sum_step(0, 1)
-    combine(3)
-    sum_step(1, 0)
-    sum_step(0, 2)
-    sum_step(1, 1)
-    sum_step(0, 3)
-    sum_step(1, 2)
-    finish(0)
-    sum_step(1, 3)
-    finish(1)
+    for u in range(NU):
+        combine(u)
+        if u > 0:
+            sum_step(u - 1, 2)
+        combine(NU + u)
+        if u > 0:
+            sum_step(u - 1, 3)
+        sum_step(u, 0)
+        if u > 0:
+            finish(u - 1)
+        sum_step(u, 1)
+    sum_step(NU - 1, 2)
+    sum_step(NU - 1, 3)
+    finish(NU - 1)
 
     for n in range(2):
-        wait(own_kv, kv_s.at[n])
-        wait(own_kv.at[0], kv2_s.at[n])
+        for d in range(2):
+            wait(kv_part(s, n), kv_s.at[d, n])
+        wait(kv_part(s, n), kv2_s.at[n])
     for n in range(4):
         wait(own_kv, kvc_s.at[n])
     for n in range(3):
@@ -533,11 +564,12 @@
     for f in range(NF):
         wait(px_v.at[f], px_s.at[f])
         wait(s_v.at[f, pl.ds(0, FIFTEEN), :], dsp_s.at[f])
+    for f in range(NR):
         wait(y_v.at[f, pl.ds(0, FIFTEEN), :], ret_s.at[f])
     wait(px2_v, px2_s)
     for d in range(2):
         wait(xg_v.at[pl.ds(0, 2), pl.ds(0, 7 * HALF_TOK), :], xg_s.at[d])
-        for u in range(2):
+        for u in range(NU):
             for n in range(far(u, d)):
                 wait(rs_s.at[u, d, n], rs_ss.at[u, d, n])
 
@@ -549,7 +581,7 @@
 
     @pl.when(giver == 1)
     def _():
-        for n in range(12):
+        for n in range(8 + NR):
             wait(mine_chunks[n][1], wz_s.at[n])
             wait(mine_chunks[n][1], wf_s.at[n])
 
@@ -590,18 +622,18 @@
             pltpu.VMEM((ROWS, FF), F32),
             pltpu.VMEM((ROWS, FF), F32),
             pltpu.VMEM((ROWS, FF), BF),
-            pltpu.VMEM((NF, ROWS, FC), BF),
-            pltpu.VMEM((NF, ROWS, FC), BF),
-            pltpu.VMEM((NF, TOKS, FC), F32),
-            pltpu.VMEM((2, 2, 4, TOK, FC), BF),
-            pltpu.VMEM((2, 2, 4, TOK, FC), BF),
-            dma((8,)), dma((3,)), dma((12,)), dma((12,)), dma((3,)), dma((12,)),
-            dma((2,)), dma((2,)), dma((4,)), dma((4,)), dma((2,)), dma((2,)),
+            pltpu.VMEM((NR, ROWS, RC), BF),
+            pltpu.VMEM((NR, ROWS, RC), BF),
+            pltpu.VMEM((NR, TOKS, RC), F32),
+            pltpu.VMEM((NU, 2, 4, TOK, RC), BF),
+            pltpu.VMEM((NU, 2, 4, TOK, RC), BF),
+            dma((8,)), dma((3,)), dma((8 + NR,)), dma((8 + NR,)), dma((3,)), dma((8 + NR,)),
+            dma((2, 2)), dma((2, 2)), dma((4,)), dma((4,)), dma((2,)), dma((2,)),
             dma((7,)), dma((7,)),
             dma, dma((2,)), dma((2,)), dma, dma((4, 2)), dma((4, 2)), dma, dma,
             dma((NF,)), dma((NF,)), dma, dma,
-            dma((2,)), dma((NF, 2, 4)), dma((NF,)), dma((NF,)), dma((NF,)), dma((NF,)), dma((NF,)), dma((NF,)),
-            dma((2, 2, 4)), dma((2, 2, 4)),
+            dma((2,)), dma((NF, 2, 4)), dma((NF,)), dma((NF,)), dma((NF,)), dma((NR,)), dma((NR,)), dma((NR,)),
+            dma((NU, 2, 4)), dma((NU, 2, 4)),
         ],
         compiler_params=pltpu.CompilerParams(
             collective_id=0, has_side_effects=True, vmem_limit_bytes=62 * 1024 * 1024

time: 201 us -> 173 us (0.86)
  Pallas kernels: 198 us -> 172 us
    pallas_call x1, Pallas kernels: 198 us -> 172 us  [per_device(): pl.pallas_call(layer_kernel, out_shape=jax.ShapeDtypeStruct((TOK, HALF_D)...]
where the time goes in v2:
time: 173 us
  Pallas kernels  172 us (99%)
    pallas_call x1, Pallas kernels, per_device(): pl.pallas_call(layer_kernel, out_shape=jax.ShapeDtypeStruct((TOK, HALF_D)...  172 us

profile of v2, /device:TPU:32, one launch (start us, length us, event | category | flops | bytes accessed | tf_op | source)
XLA Modules:
  0.0 173.2 jit_solution(10751544812569534881)
XLA Ops:
  0.0 171.5 %layer.1 = bf16[128,1024]{1,0:T(8,128)(2,1)} custom-call(bf16[128,2048]{1,0:T(8,128)(2,1)} %bitcast.19, bf16[128,256]{1,0:T(8,128)(2,1)} %bitcast.21, bf16[128,256]{1,0:T(8,128)(2,1)} %bitcast.22, bf16[128,2048]{1,0:T(8,128)(2,1)} %bitcast.20, bf16[2048,128]{1,0:T(8,128)(2,1)} %w_h.1, f32[1,1024]{1,0:T(1,128)} %bitcast.23, bf16[2048,384]{1,0:T(8,128)(2,1)} %bitcast.15, ...), custom_call_target="tpu_custom_call" | custom-call | tf_op jit(solution)/shard_map/layer/pallas_call | solution.py:594
  171.5 1.7 copy.13

commit v3 on v2

--- a/solution.py
+++ b/solution.py
@@ -22,16 +22,27 @@
 MSG = NBLK * CAP
 ROWS = NP * MSG
 TOKS = NBLK * TOK
-NF = 4
-FC = D // NF
 FFH = 384
 FF = 768
 HALF_D = D // 2
 WROWS = 1024
-NR = 8
-RC = D // NR
-NU = NR // 2
-PAIRS = tuple(h * NU + u for u in range(NU) for h in range(2))
+
+
+def starts(widths):
+    return tuple(sum(widths[:n]) for n in range(len(widths)))
+
+
+CW = (256, 512, 512, 512, 256)
+CS = starts(CW)
+NF = len(CW)
+RW = (256, 256, 256, 128, 128)
+RING_U = 4
+RS = starts(RW)
+NU = len(RW)
+PIECE = 256
+GU = 2 * (D // PIECE)
+SWAPS = GU + 2 * NU
+PAIRS = tuple((u, h) for u in range(NU) for h in range(2))
 
 
 def layer_kernel(
@@ -41,14 +52,14 @@
     attn_v, ph_v, px_v, px2_v, mix_v, mixo_v,
     xg_v, p_v, gt_v, g_v, s_v, r_v,
     wg_v, wu_v, wd_v, ag_v, au_v, hid_v,
-    y_v, yr_v, o_v, rs_s, rs_r,
+    y_v, yr_v, o_v, rs_s, rs_r, ds_v, dr_v,
     loc, hk, hz, wz_s, wk_s, wf_s,
     kv_s, kv_r, kvc_s, kvc_r, kv2_s, kv2_r,
     sm_s, sm_r,
     wa_s, wa_r, wa2_r, wb_s, wb_r, wb2_r, wc_s, wc_r,
     px_s, px_r, px2_s, px2_r,
     xg_s, xg_r, dsp_s, dsp_r, dsp_l, ret_s, ret_r, ret_l,
-    rs_ss, rs_rs,
+    rs_ss, rs_rs, ds_s, ds_r,
 ):
     rem, div = lax.rem, lax.div
     s = lax.axis_index("seq")
@@ -125,9 +136,10 @@
     def greet(who):
         pl.semaphore_signal(barrier, inc=1, device_id=who, device_id_type=MESH)
 
-    for who in (other, partner, cross, zh_next, zh_prev, zh_opp):
+    for who in (other, cross):
         greet(who)
-    greet(dev(zmod(z - 1 + 2 * t), e, c))
+    for k in range(1, NZ):
+        greet(dev(zmod(z + k), e, c))
 
     def greet_plane(k, carry):
         greet(dev(z, plane_peer(k), c))
@@ -140,7 +152,7 @@
     wait(gain_v.at[:, pl.ds(gcol, HALF_D)], loc.at[5])
     wait(ids_v.at[:, pl.ds(icol, TOK)], loc.at[6])
     wait(gat_v.at[:, pl.ds(icol, TOK)], loc.at[7])
-    pl.semaphore_wait(barrier, 7 + NP - 1)
+    pl.semaphore_wait(barrier, 2 + NZ - 1 + NP - 1)
 
     def kv_part(i, n):
         return kv_v.at[i, n]
@@ -166,9 +178,9 @@
     send(mine, mine, wb_s, wb_r.at[0, 0], b_next)
     send(mine, mine, wb_s, wb_r.at[0, 1], b_prev)
 
-    def on_chip(i):
-        part = wpart(i, 0, WROWS)
-        send(part, part, wc_s, wc_r, other)
+    def on_chip(n, m):
+        part = wpart(blk(OFF[n], OFF[m]), 0, WROWS)
+        send(part, part, wc_s, wc_r.at[n, m], other)
 
     def spread_b(n):
         part = wpart(blk(OFF[n], 0), 0, WROWS)
@@ -206,8 +218,8 @@
     send(part, part, wa_s, wa2_r.at[1], a_prev)
     spread_b(1)
     spread_b(2)
-    on_chip(blk(3, 0))
-    on_chip(blk(1, 0))
+    on_chip(1, 0)
+    on_chip(2, 0)
 
     wait(kv_part(left, 1), kv_r.at[0, 1])
     send(kv_v.at[left], kv_v.at[left], kvc_s.at[1], kvc_r.at[1], other)
@@ -217,11 +229,13 @@
     def wchunks(h):
         col = m8(h * FFH, 128)
         out = []
-        for f in range(NF):
-            out.append((wg_h.at[pl.ds(f * FC, FC), :], wg_v.at[pl.ds(f * FC, FC), pl.ds(col, FFH)]))
-            out.append((wu_h.at[pl.ds(f * FC, FC), :], wu_v.at[pl.ds(f * FC, FC), pl.ds(col, FFH)]))
-        for f in PAIRS:
-            out.append((wd_h.at[:, pl.ds(f * RC, RC)], wd_v.at[pl.ds(col, FFH), pl.ds(f * RC, RC)]))
+        for lo in range(0, D, PIECE):
+            rows = pl.ds(lo, PIECE)
+            out.append((wg_h.at[rows, :], wg_v.at[rows, pl.ds(col, FFH)]))
+            out.append((wu_h.at[rows, :], wu_v.at[rows, pl.ds(col, FFH)]))
+        for u, h in PAIRS:
+            cols = pl.ds(h * HALF_D + RS[u], RW[u])
+            out.append((wd_h.at[:, cols], wd_v.at[pl.ds(col, FFH), cols]))
         return out
 
     mine_chunks = wchunks(t)
@@ -245,29 +259,28 @@
     wait(wpart(blk(2, 0), 0, 512), wa2_r.at[0])
     wait(wpart(blk(2, 0), 512, 512), wa2_r.at[1])
     spread_b(3)
-    on_chip(blk(2, 0))
+    on_chip(3, 0)
 
     def second_axis(n):
         wait(mine, wb_r.at[n, 0])
         fwd = wpart(blk(OFF[n], 3), 0, 512)
         send(fwd, fwd, wb_s, wb2_r.at[n, 0], b_next)
-        on_chip(blk(OFF[n], 3))
+        on_chip(n, 1)
         wait(mine, wb_r.at[n, 1])
         fwd = wpart(blk(OFF[n], 1), 512, 512)
         send(fwd, fwd, wb_s, wb2_r.at[n, 1], b_prev)
-        on_chip(blk(OFF[n], 1))
+        on_chip(n, 2)
 
     def second_axis_end(n):
         wait(wpart(blk(OFF[n], 2), 0, 512), wb2_r.at[n, 0])
         wait(wpart(blk(OFF[n], 2), 512, 512), wb2_r.at[n, 1])
-        on_chip(blk(OFF[n], 2))
+        on_chip(n, 3)
 
     second_axis(0)
 
     wait(kv_part(opp, 0), kv2_r.at[0])
     wait(kv_part(opp, 1), kv2_r.at[1])
     send(kv_v.at[opp], kv_v.at[opp], kvc_s.at[3], kvc_r.at[3], other)
-    swap(0, 4)
 
     for n in range(3):
         wait(ids_v.at[:, pl.ds(icol, TOK)], sm_r.at[n])
@@ -338,44 +351,54 @@
             second_axis(3)
         if grp == 2:
             second_axis_end(1)
-    second_axis_end(2)
-    second_axis_end(3)
-    wait(w_v.at[pl.ds(0, 15), pl.ds(0, WROWS), :], wc_r)
 
     my_row = m8(t * HALF_TOK, HALF_TOK)
     their_row = m8((1 - t) * HALF_TOK, HALF_TOK)
-    for f in range(NF):
-
-        def project(i, carry):
-            wb = f * 4 + i * 2
-            ww = jnp.concatenate([w_v[wb], w_v[wb + 1]], axis=1)
-            r = jnp.dot(attn_v[...], ww, preferred_element_type=F32)
-            ph_v[f, :, pl.ds(m8(i * 256, 256), 256)] = r.astype(BF)
-            return carry
-
-        lax.fori_loop(0, 2, project, 0)
-        send(ph_v.at[f, pl.ds(their_row, HALF_TOK), :], px_v.at[f], px_s.at[f], px_r.at[f], partner)
+
+    def project(n, m):
+        i = blk(OFF[n], OFF[m])
+        if n + m > 0:
+            wait(mine, wc_r.at[m, n])
+        ph_v[i] = jnp.dot(attn_v[...], w_v[i], preferred_element_type=F32).astype(BF)
+        send(ph_v.at[i, pl.ds(their_row, HALF_TOK), :], px_v.at[i], px_s, px_r, partner)
+
+    for n in range(3):
+        for m in range(3):
+            project(n, m)
+    project(3, 0)
+    project(0, 3)
+    project(1, 3)
+    project(3, 1)
+    second_axis_end(2)
+    project(2, 3)
+    project(3, 2)
+    second_axis_end(3)
+    project(3, 3)
+    swap(0, 2)
     wait(x_v, loc.at[4])
     wait(gain_v.at[:, pl.ds(gcol, HALF_D)], sm_r.at[6])
+    wait(px_v, px_r)
     power = jnp.zeros((HALF_TOK, 1), F32)
-    for f in range(NF):
-        wait(px_v.at[f], px_r.at[f])
+    for i in range(NP):
         mix = (
-            x_v[pl.ds(my_row, HALF_TOK), f * FC : (f + 1) * FC].astype(F32)
-            + ph_v[f, pl.ds(my_row, HALF_TOK), :].astype(F32)
-            + px_v[f].astype(F32)
+            x_v[pl.ds(my_row, HALF_TOK), i * 128 : (i + 1) * 128].astype(F32)
+            + ph_v[i, pl.ds(my_row, HALF_TOK), :].astype(F32)
+            + px_v[i].astype(F32)
         )
-        mix_v[f] = mix
+        mix_v[:, i * 128 : (i + 1) * 128] = mix
         power = power + jnp.sum(mix * mix, axis=1, keepdims=True)
     inverse = lax.rsqrt(power / D + 1e-06)
 
     zrow = m8(z * HALF_TOK, HALF_TOK)
+    def cols_of(f):
+        return pl.ds(CS[f], CW[f])
+
     def ring_open(f):
-        gain = gain_v[:, f * FC : (f + 1) * FC]
-        xg_v[f, pl.ds(zrow, HALF_TOK), :] = (mix_v[f] * inverse * gain).astype(BF)
-        shard = xg_v.at[f, pl.ds(zrow, HALF_TOK), :]
-        send(shard, shard, xg_s.at[0], xg_r.at[f, 0, 0], z_next)
-        send(shard, shard, xg_s.at[1], xg_r.at[f, 1, 0], z_prev)
+        cols = cols_of(f)
+        xg_v[pl.ds(zrow, HALF_TOK), cols] = (mix_v[:, cols] * inverse * gain_v[:, cols]).astype(BF)
+        shard = xg_v.at[pl.ds(zrow, HALF_TOK), cols]
+        send(shard, shard, xg_s.at[f, 0], xg_r.at[f, 0, 0], z_next)
+        send(shard, shard, xg_s.at[f, 1], xg_r.at[f, 1, 0], z_prev)
 
     def reach(f, d):
         return 4 if (f + d) % 2 == 0 else 3
@@ -385,42 +408,49 @@
             if k > reach(f, d):
                 continue
             src_z = zmod(z - k) if d == 0 else zmod(z + k)
-            shard = xg_v.at[f, pl.ds(m8(src_z * HALF_TOK, HALF_TOK), HALF_TOK), :]
+            shard = xg_v.at[pl.ds(m8(src_z * HALF_TOK, HALF_TOK), HALF_TOK), cols_of(f)]
             wait(shard, xg_r.at[f, d, k - 1])
             if k + 1 <= reach(f, d):
-                send(shard, shard, xg_s.at[d], xg_r.at[f, d, k], z_next if d == 0 else z_prev)
+                send(shard, shard, xg_s.at[f, d], xg_r.at[f, d, k], z_next if d == 0 else z_prev)
 
     my_slot = pl.ds(m8(e * MSG, 16), MSG)
 
-    def exchange(buf, dst, f, ss, rs, ls):
+    def exchange(buf, dst, cols, ss, rs, ls, lo, hi):
         def one(k, carry):
             peer = plane_peer(k)
             send(
-                buf.at[f, pl.ds(m8(peer * MSG, 16), MSG), :],
-                dst.at[f, my_slot, :],
-                ss.at[f],
-                rs.at[f],
+                buf.at[pl.ds(m8(peer * MSG, 16), MSG), cols],
+                dst.at[my_slot, cols],
+                ss,
+                rs,
                 dev(z, peer, c),
             )
             return carry
 
-        lax.fori_loop(1, NP, one, 0)
-        local(buf.at[f, my_slot, :], dst.at[f, my_slot, :], ls.at[f])
-
-    FIFTEEN = (NP - 1) * MSG
-
-    def exchanged(dst, f, rs, ls):
-        wait(dst.at[f, pl.ds(0, FIFTEEN), :], rs.at[f])
-        wait(dst.at[f, my_slot, :], ls.at[f])
+        parts = hi - lo + 1
+        for n in range(parts):
+            lax.fori_loop(1 + n * (NP - 1) // parts, 1 + (n + 1) * (NP - 1) // parts, one, 0)
+            if n < parts - 1:
+                swap(lo + n, lo + n + 1)
+        local(buf.at[my_slot, cols], dst.at[my_slot, cols], ls)
+
+    FIFTEEN = pl.ds(0, (NP - 1) * MSG)
+
+    def exchanged(dst, cols, rs, ls):
+        wait(dst.at[FIFTEEN, cols], rs)
+        wait(dst.at[my_slot, cols], ls)
 
     def pick_rows(f):
+        cols = cols_of(f)
+
         def group(i, carry):
             rows = pl.ds(m8(i * 256, 256), 256)
-            s_v[f, rows, :] = jnp.dot(p_v[rows, :], xg_v[f], preferred_element_type=F32).astype(BF)
+            s_v[rows, cols] = jnp.dot(p_v[rows, :], xg_v[:, cols], preferred_element_type=F32).astype(BF)
             return carry
 
         lax.fori_loop(0, ROWS // 256, group, 0)
-        exchange(s_v, r_v, f, dsp_s, dsp_r, dsp_l)
+        lo, hi = ((2, 4), (4, 8), (8, 12), (12, GU), (GU, GU + 2))[f]
+        exchange(s_v, r_v, cols, dsp_s.at[f], dsp_r.at[f], dsp_l.at[f], lo, hi)
 
     ring_open(0)
     ring_open(1)
@@ -430,37 +460,24 @@
                 ring_step(f, wave - f)
         if wave + 1 < NF:
             ring_open(wave + 1)
-        if wave == NF + 3:
-            their_f = (1 - t) * 2
-            mid = ph_v.at[pl.ds(their_f, 2), pl.ds(my_row, HALF_TOK), :]
-            send(mid, px2_v, px2_s, px2_r, partner)
-            swap(4, 8 + NR)
         if wave >= 4:
             pick_rows(wave - 4)
-
-    wait(px2_v, px2_r)
-    my_f = t * 2
-    for u in range(2):
-        cols = pl.ds(m8(gcol + u * FC, FC), FC)
-        mixo_v[u, pl.ds(my_row, HALF_TOK), :] = mix_v[my_f + u]
-        mixo_v[u, pl.ds(their_row, HALF_TOK), :] = (
-            x_v[pl.ds(their_row, HALF_TOK), cols].astype(F32)
-            + ph_v[my_f + u, pl.ds(their_row, HALF_TOK), :].astype(F32)
-            + px2_v[u].astype(F32)
-        )
+    mid = ph_v.at[pl.ds((1 - t) * 8, 8), pl.ds(my_row, HALF_TOK), :]
+    send(mid, px2_v, px2_s, px2_r, partner)
 
     wait(wg_v.at[:, pl.ds(hcol, FFH)], hk.at[0])
     wait(wu_v.at[:, pl.ds(hcol, FFH)], hk.at[1])
     for f in range(NF):
-        weights_in(2 * f)
-        weights_in(2 * f + 1)
-        exchanged(r_v, f, dsp_r, dsp_l)
+        for n in range(2 * (CS[f] // PIECE), 2 * ((CS[f] + CW[f]) // PIECE)):
+            weights_in(n)
+        exchanged(r_v, cols_of(f), dsp_r.at[f], dsp_l.at[f])
+        lo, hi = CS[f], CS[f] + CW[f]
 
         def gate_up(i, carry):
             rows = pl.ds(m8(i * 256, 256), 256)
-            rr = r_v[f, rows, :]
-            ga = jnp.dot(rr, wg_v[f * FC : (f + 1) * FC, :], preferred_element_type=F32)
-            ua = jnp.dot(rr, wu_v[f * FC : (f + 1) * FC, :], preferred_element_type=F32)
+            rr = r_v[rows, lo:hi]
+            ga = jnp.dot(rr, wg_v[lo:hi, :], preferred_element_type=F32)
+            ua = jnp.dot(rr, wu_v[lo:hi, :], preferred_element_type=F32)
             if f > 0:
                 ga = ga + ag_v[rows, :]
                 ua = ua + au_v[rows, :]
@@ -474,37 +491,65 @@
         lax.fori_loop(0, ROWS // 256, gate_up, 0)
 
     wait(wd_v.at[pl.ds(hcol, FFH), :], hk.at[2])
-    for n, f in enumerate(PAIRS):
-        weights_in(8 + n)
-
-        def down(i, carry):
+    def pair_cols(u, h):
+        return pl.ds(h * HALF_D + RS[u], RW[u])
+
+    def down(n):
+        u, h = PAIRS[n]
+        weights_in(GU + n)
+        cols = pair_cols(u, h)
+
+        def group(i, carry):
             rows = pl.ds(m8(i * 256, 256), 256)
-            cols = slice(f * RC, (f + 1) * RC)
             y0 = jnp.dot(hid_v[rows, :FFH], wd_v[:FFH, cols], preferred_element_type=F32)
             y1 = jnp.dot(hid_v[rows, FFH:], wd_v[FFH:, cols], preferred_element_type=F32)
-            y_v[f, rows, :] = (y0.astype(BF).astype(F32) + y1.astype(BF).astype(F32)).astype(BF)
+            y_v[rows, cols] = (y0.astype(BF).astype(F32) + y1.astype(BF).astype(F32)).astype(BF)
             return carry
 
-        lax.fori_loop(0, ROWS // 256, down, 0)
-        exchange(y_v, yr_v, f, ret_s, ret_r, ret_l)
-
-    def combine(f):
-        exchanged(yr_v, f, ret_r, ret_l)
+        lax.fori_loop(0, ROWS // 256, group, 0)
+
+    def give_back(n):
+        u, h = PAIRS[n]
+        lo = GU + n + 2
+        hi = min(lo + 1, SWAPS)
+        lo = min(lo, hi)
+        exchange(y_v, yr_v, pair_cols(u, h), ret_s.at[u, h], ret_r.at[u, h], ret_l.at[u, h], lo, hi)
+
+    down(0)
+    give_back(0)
+    down(1)
+    give_back(1)
+
+    wait(px2_v, px2_r)
+    mixo_v[pl.ds(my_row, HALF_TOK), :] = mix_v[:, pl.ds(gcol, HALF_D)]
+    for i in range(8):
+        cols = pl.ds(m8(gcol + i * 128, 128), 128)
+        mixo_v[pl.ds(their_row, HALF_TOK), i * 128 : (i + 1) * 128] = (
+            x_v[pl.ds(their_row, HALF_TOK), cols].astype(F32)
+            + ph_v[t * 8 + i, pl.ds(their_row, HALF_TOK), :].astype(F32)
+            + px2_v[i].astype(F32)
+        )
+
+    def combine(u, h):
+        cols = pair_cols(u, h)
+        exchanged(yr_v, cols, ret_r.at[u, h], ret_l.at[u, h])
 
         def group(i, carry):
             rows = pl.ds(m8(i * 256, 256), 256)
-            o_v[f, rows, :] = jnp.dot(g_v[rows, :], yr_v[f], preferred_element_type=F32)
+            o_v[rows, cols] = jnp.dot(g_v[rows, :], yr_v[:, cols], preferred_element_type=F32)
             return carry
 
         lax.fori_loop(0, TOKS // 256, group, 0)
 
     def own_part(dest, u):
-        return o_v[rem(dest, 2) * NU + u, pl.ds(m8(div(dest, 2) * TOK, TOK), TOK), :]
+        cols = pl.ds(m8(rem(dest, 2) * HALF_D + RS[u], 128), RW[u])
+        return o_v[pl.ds(m8(div(dest, 2) * TOK, TOK), TOK), cols]
 
     def far(u, d):
         return 4 if (u + d) % 2 == 0 else 3
 
     def sum_step(u, i):
+        cols = pl.ds(RS[u], RW[u])
         for d in range(2):
             dist = far(u, d) - i
             if dist < 1:
@@ -512,41 +557,63 @@
             dest = zmod(z + dist) if d == 0 else zmod(z - dist)
             part = own_part(dest, u)
             if i > 0:
-                slot = rs_r.at[u, d, dist]
-                wait(slot, rs_rs.at[u, d, dist])
-                part = part + rs_r[u, d, dist].astype(F32)
-            rs_s[u, d, dist - 1] = part.astype(BF)
+                wait(rs_r.at[d, dist, :, cols], rs_rs.at[u, d, dist])
+                part = part + rs_r[d, dist, :, cols].astype(F32)
+            rs_s[d, dist - 1, :, cols] = part.astype(BF)
             send(
-                rs_s.at[u, d, dist - 1],
-                rs_r.at[u, d, dist - 1],
+                rs_s.at[d, dist - 1, :, cols],
+                rs_r.at[d, dist - 1, :, cols],
                 rs_ss.at[u, d, dist - 1],
                 rs_rs.at[u, d, dist - 1],
                 z_next if d == 0 else z_prev,
             )
 
+    FAR_FIRST = (4, 3, 5, 2, 6, 1, 7)
+
+    def send_sums(u):
+        for k in FAR_FIRST:
+            dest = zmod(z + k)
+            ds_v[u - RING_U, k - 1] = own_part(dest, u).astype(BF)
+            send(
+                ds_v.at[u - RING_U, k - 1],
+                dr_v.at[u - RING_U, k - 1],
+                ds_s.at[u - RING_U],
+                ds_r.at[u - RING_U],
+                dev(dest, e, c),
+            )
+
     def finish(u):
-        for d in range(2):
-            wait(rs_r.at[u, d, 0], rs_rs.at[u, d, 0])
-        lo = (u % 2) * RC
-        out_ref[:, u * RC : (u + 1) * RC] = (
-            mixo_v[u // 2, :, lo : lo + RC]
-            + (own_part(z, u) + rs_r[u, 0, 0].astype(F32) + rs_r[u, 1, 0].astype(F32))
-        ).astype(BF)
-
-    for u in range(NU):
-        combine(u)
-        if u > 0:
-            sum_step(u - 1, 2)
-        combine(NU + u)
-        if u > 0:
-            sum_step(u - 1, 3)
-        sum_step(u, 0)
-        if u > 0:
-            finish(u - 1)
-        sum_step(u, 1)
-    sum_step(NU - 1, 2)
-    sum_step(NU - 1, 3)
-    finish(NU - 1)
+        cols = pl.ds(RS[u], RW[u])
+        total = own_part(z, u)
+        if u < RING_U:
+            for d in range(2):
+                wait(rs_r.at[d, 0, :, cols], rs_rs.at[u, d, 0])
+                total = total + rs_r[d, 0, :, cols].astype(F32)
+        else:
+            wait(dr_v.at[u - RING_U], ds_r.at[u - RING_U])
+            for k in range(NZ - 1):
+                total = total + dr_v[u - RING_U, k].astype(F32)
+        out_ref[:, cols] = (mixo_v[:, cols] + total).astype(BF)
+
+    last = 2 * NU
+    for n in range(2, last + 4):
+        if n < last:
+            down(n)
+        if n - 2 < last:
+            combine(*PAIRS[n - 2])
+        for u in range(NU):
+            i = n - (2 * u + 3)
+            if u >= RING_U:
+                if i == 0:
+                    send_sums(u)
+            elif 0 <= i < 4:
+                sum_step(u, i)
+            elif i == 4:
+                finish(u)
+        if n < last:
+            give_back(n)
+    for u in range(RING_U, NU):
+        finish(u)
 
     for n in range(2):
         for d in range(2):
@@ -561,17 +628,20 @@
     wait(w_v.at[pl.ds(0, 3), pl.ds(0, WROWS), :], wa_s)
     wait(w_v.at[pl.ds(0, 12), pl.ds(0, WROWS), :], wb_s)
     wait(w_v.at[pl.ds(0, 15), pl.ds(0, WROWS), :], wc_s)
+    wait(px_v, px_s)
     for f in range(NF):
-        wait(px_v.at[f], px_s.at[f])
-        wait(s_v.at[f, pl.ds(0, FIFTEEN), :], dsp_s.at[f])
-    for f in range(NR):
-        wait(y_v.at[f, pl.ds(0, FIFTEEN), :], ret_s.at[f])
+        wait(s_v.at[FIFTEEN, cols_of(f)], dsp_s.at[f])
+        for d in range(2):
+            wait(xg_v.at[pl.ds(0, reach(f, d) * HALF_TOK), cols_of(f)], xg_s.at[f, d])
     wait(px2_v, px2_s)
-    for d in range(2):
-        wait(xg_v.at[pl.ds(0, 2), pl.ds(0, 7 * HALF_TOK), :], xg_s.at[d])
-        for u in range(NU):
-            for n in range(far(u, d)):
-                wait(rs_s.at[u, d, n], rs_ss.at[u, d, n])
+    for u in range(NU):
+        for h in range(2):
+            wait(y_v.at[FIFTEEN, pair_cols(u, h)], ret_s.at[u, h])
+        for d in range(2):
+            for n in range(far(u, d) if u < RING_U else 0):
+                wait(rs_s.at[d, n, :, pl.ds(RS[u], RW[u])], rs_ss.at[u, d, n])
+        if u >= RING_U:
+            wait(ds_v.at[u - RING_U], ds_s.at[u - RING_U])
 
     @pl.when(giver == 0)
     def _():
@@ -581,7 +651,7 @@
 
     @pl.when(giver == 1)
     def _():
-        for n in range(8 + NR):
+        for n in range(SWAPS):
             wait(mine_chunks[n][1], wz_s.at[n])
             wait(mine_chunks[n][1], wf_s.at[n])
 
@@ -605,35 +675,38 @@
             pltpu.VMEM((8, TOKS), jnp.int32),
             pltpu.VMEM((8, TOKS), F32),
             pltpu.VMEM((TOK, D), BF),
-            pltpu.VMEM((NF, TOK, FC), BF),
-            pltpu.VMEM((NF, HALF_TOK, FC), BF),
-            pltpu.VMEM((2, HALF_TOK, FC), BF),
-            pltpu.VMEM((NF, HALF_TOK, FC), F32),
-            pltpu.VMEM((2, TOK, FC), F32),
-            pltpu.VMEM((NF, TOKS, FC), BF),
+            pltpu.VMEM((NP, TOK, 128), BF),
+            pltpu.VMEM((NP, HALF_TOK, 128), BF),
+            pltpu.VMEM((8, HALF_TOK, 128), BF),
+            pltpu.VMEM((HALF_TOK, D), F32),
+            pltpu.VMEM((TOK, HALF_D), F32),
+            pltpu.VMEM((TOKS, D), BF),
             pltpu.VMEM((ROWS, TOKS), BF),
             pltpu.VMEM((ROWS, TOKS), F32),
             pltpu.VMEM((TOKS, ROWS), BF),
-            pltpu.VMEM((NF, ROWS, FC), BF),
-            pltpu.VMEM((NF, ROWS, FC), BF),
+            pltpu.VMEM((ROWS, D), BF),
+            pltpu.VMEM((ROWS, D), BF),
             pltpu.VMEM((D, FF), BF),
             pltpu.VMEM((D, FF), BF),
             pltpu.VMEM((FF, D), BF),
             pltpu.VMEM((ROWS, FF), F32),
             pltpu.VMEM((ROWS, FF), F32),
             pltpu.VMEM((ROWS, FF), BF),
-            pltpu.VMEM((NR, ROWS, RC), BF),
-            pltpu.VMEM((NR, ROWS, RC), BF),
-            pltpu.VMEM((NR, TOKS, RC), F32),
-            pltpu.VMEM((NU, 2, 4, TOK, RC), BF),
-            pltpu.VMEM((NU, 2, 4, TOK, RC), BF),
-            dma((8,)), dma((3,)), dma((8 + NR,)), dma((8 + NR,)), dma((3,)), dma((8 + NR,)),
+            pltpu.VMEM((ROWS, D), BF),
+            pltpu.VMEM((ROWS, D), BF),
+            pltpu.VMEM((TOKS, D), F32),
+            pltpu.VMEM((2, 4, TOK, HALF_D), BF),
+            pltpu.VMEM((2, 4, TOK, HALF_D), BF),
+            pltpu.VMEM((NU - RING_U, NZ - 1, TOK, 128), BF),
+            pltpu.VMEM((NU - RING_U, NZ - 1, TOK, 128), BF),
+            dma((8,)), dma((3,)), dma((SWAPS,)), dma((SWAPS,)), dma((3,)), dma((SWAPS,)),
             dma((2, 2)), dma((2, 2)), dma((4,)), dma((4,)), dma((2,)), dma((2,)),
             dma((7,)), dma((7,)),
-            dma, dma((2,)), dma((2,)), dma, dma((4, 2)), dma((4, 2)), dma, dma,
-            dma((NF,)), dma((NF,)), dma, dma,
-            dma((2,)), dma((NF, 2, 4)), dma((NF,)), dma((NF,)), dma((NF,)), dma((NR,)), dma((NR,)), dma((NR,)),
-            dma((NU, 2, 4)), dma((NU, 2, 4)),
+            dma, dma((2,)), dma((2,)), dma, dma((4, 2)), dma((4, 2)), dma, dma((4, 4)),
+            dma, dma, dma, dma,
+            dma((NF, 2)), dma((NF, 2, 4)), dma((NF,)), dma((NF,)), dma((NF,)),
+            dma((NU, 2)), dma((NU, 2)), dma((NU, 2)),
+            dma((NU, 2, 4)), dma((NU, 2, 4)), dma((NU - RING_U,)), dma((NU - RING_U,)),
         ],
         compiler_params=pltpu.CompilerParams(
             collective_id=0, has_side_effects=True, vmem_limit_bytes=62 * 1024 * 1024

time: 173 us -> 166 us (0.960)
  Pallas kernels: 172 us -> 164 us
    pallas_call x1, Pallas kernels: 172 us -> 164 us  [per_device(): pl.pallas_call(layer_kernel, out_shape=jax.ShapeDtypeStruct((TOK, HALF_D)...]
where the time goes in v3:
time: 166 us
  Pallas kernels  164 us (99%)
  local copies, waits for them, and re-layouts  1.67 us (1%)
    pallas_call x1, Pallas kernels, per_device(): pl.pallas_call(layer_kernel, out_shape=jax.ShapeDtypeStruct((TOK, HALF_D)...  164 us

profile of v3, /device:TPU:32, one launch (start us, length us, event | category | flops | bytes accessed | tf_op | source)
XLA Modules:
  0.0 165.6 jit_solution(4496190855625353736)
XLA Ops:
  0.0 163.9 %layer.1 = bf16[128,1024]{1,0:T(8,128)(2,1)} custom-call(bf16[128,2048]{1,0:T(8,128)(2,1)} %bitcast.19, bf16[128,256]{1,0:T(8,128)(2,1)} %bitcast.21, bf16[128,256]{1,0:T(8,128)(2,1)} %bitcast.22, bf16[128,2048]{1,0:T(8,128)(2,1)} %bitcast.20, bf16[2048,128]{1,0:T(8,128)(2,1)} %w_h.1, f32[1,1024]{1,0:T(1,128)} %bitcast.23, bf16[2048,384]{1,0:T(8,128)(2,1)} %bitcast.15, ...), custom_call_target="tpu_custom_call" | custom-call | tf_op jit(solution)/shard_map/layer/pallas_call | solution.py:664
  163.9 1.7 %copy.13 = bf16[1,128,1024]{2,1,0:T(8,128)(2,1)} copy(bf16[1,128,1024]{2,1,0:T(8,128)(2,1)} %bitcast.18) | data formatting | bytes 524288

commit v4 on v3

--- a/solution.py
+++ b/solution.py
@@ -35,7 +35,7 @@
 CW = (256, 512, 512, 512, 256)
 CS = starts(CW)
 NF = len(CW)
-RW = (256, 256, 256, 128, 128)
+RW = (128, 256, 256, 256, 128)
 RING_U = 4
 RS = starts(RW)
 NU = len(RW)
@@ -449,7 +449,7 @@
             return carry
 
         lax.fori_loop(0, ROWS // 256, group, 0)
-        lo, hi = ((2, 4), (4, 8), (8, 12), (12, GU), (GU, GU + 2))[f]
+        lo, hi = ((2, 4), (4, 8), (8, 12), (12, GU), (GU, GU + 3))[f]
         exchange(s_v, r_v, cols, dsp_s.at[f], dsp_r.at[f], dsp_l.at[f], lo, hi)
 
     ring_open(0)
@@ -510,7 +510,7 @@
 
     def give_back(n):
         u, h = PAIRS[n]
-        lo = GU + n + 2
+        lo = GU + n + 3
         hi = min(lo + 1, SWAPS)
         lo = min(lo, hi)
         exchange(y_v, yr_v, pair_cols(u, h), ret_s.at[u, h], ret_r.at[u, h], ret_l.at[u, h], lo, hi)
@@ -519,6 +519,8 @@
     give_back(0)
     down(1)
     give_back(1)
+    down(2)
+    give_back(2)
 
     wait(px2_v, px2_r)
     mixo_v[pl.ds(my_row, HALF_TOK), :] = mix_v[:, pl.ds(gcol, HALF_D)]
@@ -532,7 +534,6 @@
 
     def combine(u, h):
         cols = pair_cols(u, h)
-        exchanged(yr_v, cols, ret_r.at[u, h], ret_l.at[u, h])
 
         def group(i, carry):
             rows = pl.ds(m8(i * 256, 256), 256)
@@ -596,13 +597,9 @@
         out_ref[:, cols] = (mixo_v[:, cols] + total).astype(BF)
 
     last = 2 * NU
-    for n in range(2, last + 4):
-        if n < last:
-            down(n)
-        if n - 2 < last:
-            combine(*PAIRS[n - 2])
-        for u in range(NU):
-            i = n - (2 * u + 3)
+    for n in range(2, last + 5):
+        for u in reversed(range(NU)):
+            i = n - (2 * u + 4)
             if u >= RING_U:
                 if i == 0:
                     send_sums(u)
@@ -610,8 +607,15 @@
                 sum_step(u, i)
             elif i == 4:
                 finish(u)
-        if n < last:
-            give_back(n)
+        if n + 1 < last:
+            down(n + 1)
+        if n - 2 < last:
+            u, h = PAIRS[n - 2]
+            exchanged(yr_v, pair_cols(u, h), ret_r.at[u, h], ret_l.at[u, h])
+        if n + 1 < last:
+            give_back(n + 1)
+        if n - 2 < last:
+            combine(*PAIRS[n - 2])
     for u in range(RING_U, NU):
         finish(u)
 

time: 166 us -> 160 us (0.964)
  Pallas kernels: 164 us -> 158 us
    pallas_call x1, Pallas kernels: 164 us -> 158 us  [per_device(): pl.pallas_call(layer_kernel, out_shape=jax.ShapeDtypeStruct((TOK, HALF_D)...]
where the time goes in v4:
time: 160 us
  Pallas kernels  158 us (99%)
  local copies, waits for them, and re-layouts  1.67 us (1%)
    pallas_call x1, Pallas kernels, per_device(): pl.pallas_call(layer_kernel, out_shape=jax.ShapeDtypeStruct((TOK, HALF_D)...  158 us

profile of v4, /device:TPU:32, one launch (start us, length us, event | category | flops | bytes accessed | tf_op | source)
XLA Modules:
  0.0 159.5 jit_solution(1964804286270903860)
XLA Ops:
  0.0 157.8 %layer.1 = bf16[128,1024]{1,0:T(8,128)(2,1)} custom-call(bf16[128,2048]{1,0:T(8,128)(2,1)} %bitcast.19, bf16[128,256]{1,0:T(8,128)(2,1)} %bitcast.21, bf16[128,256]{1,0:T(8,128)(2,1)} %bitcast.22, bf16[128,2048]{1,0:T(8,128)(2,1)} %bitcast.20, bf16[2048,128]{1,0:T(8,128)(2,1)} %w_h.1, f32[1,1024]{1,0:T(1,128)} %bitcast.23, bf16[2048,384]{1,0:T(8,128)(2,1)} %bitcast.15, ...), custom_call_target="tpu_custom_call" | custom-call | tf_op jit(solution)/shard_map/layer/pallas_call | solution.py:668
  157.8 1.7 %copy.13 = bf16[1,128,1024]{2,1,0:T(8,128)(2,1)} copy(bf16[1,128,1024]{2,1,0:T(8,128)(2,1)} %bitcast.18) | data formatting | bytes 524288
